TPU v7x, 128 devices: a whole 4x4x4 slice. The times are simulated.
128 devices in a mesh: region: 8 (over x, core), blk: 16 (over y, z).
Axes of the slice: x: 4, y: 4, z: 4, core: 2. Of those that a mesh axis runs over, the one named last changes fastest.
Arguments:
- velocity: float32 [3, 128, 512, 256], P(None, 'region', 'blk'), may hold values from -5 to 5
- viscosity: float32 [128, 512, 256], P('region', 'blk'), may hold values from 0.02 to 0.1
- match_cell: int32 [131072], P(('region', 'blk')), may hold values from 0 to 131071
- wall_cell: int32 [131072], P(('region', 'blk')), may hold values from 0 to 131071
- match_dest: int32 [131072, 1], P(('region', 'blk')), may hold values from 0 to 127; in each aligned block of 1024 rows (0 to 1023, 1024 to 2047, ...) at most 16 rows name the same one
- match_count: int32 [128], P(('region', 'blk')), may hold values from 1 to 1024, 104857 in all
- wall_geom: float32 [4, 262144], P(None, ('region', 'blk')), may hold values from -1 to 1, as said below
Outputs:
- advanced: float32 [3, 128, 512, 256], P(None, 'region', 'blk')
- wall_log_stress: float32 [131072], P(('region', 'blk'))
Inputs may be any that keep to these rules, and one draw needn't show every extreme that they name: `match_dest`: among the 1024 rows of one device at most 16 name the same owner, and some device reaches 16. The first match_count rows of a device's matching points are live; some device has all 1024 live. `match_cell`: local cell index of the device's 16 x 32 x 256 cells. `wall_cell`: local cell index of the device's 16 x 32 x 256 cells. `wall_geom`: row 0 lies in 0.02 to 0.3; rows 1 to 3 have magnitudes 0.3 to 1.
All inputs are finite; a program needn't handle non-finite values.
Results may differ from a plain program's by a relative error of at most 0.0003.
Values sent between devices are 32-bit elements; how exact they have to be, the bound alone decides.
No kernel may reach another device: no remote copies, remote signals or barrier semaphores. Data moves between devices by JAX's collectives and lax.ppermute only.
A program may use at most 192 MiB of HBM per device.

v0:
```python
import jax
import jax.numpy as jnp
from jax import lax
from jax.experimental import pallas as pl
from jax.experimental.pallas import tpu as pltpu
from jax.sharding import PartitionSpec as P

NEWTON = 2

KAPPA = 0.41
DAMPING = 26.0
NU_WALL = 0.0002
WALL_DY = 0.0005
TIME_STEP = 0.1
SPEED_FLOOR = 0.5
GUESS_RATIO = 14.0
ETAS = 32
PIECES = 3
F32 = jnp.float32
BF16 = jnp.bfloat16


def pieces_of(values, count):
    parts = []
    rest = values
    for index in range(count):
        part = rest.astype(BF16)
        parts.append(part)
        if index + 1 < count:
            rest = rest - part.astype(F32)
    return parts


def as_row(block):
    rows = block.shape[0]
    return jnp.concatenate([block[i : i + 1, :] for i in range(rows)], axis=1)


def row_iota(shape):
    return lax.broadcasted_iota(jnp.int32, shape, 0)


def fill_padded(padded, field_ref, xlo_ref, xhi_ref, ylo_ref, yhi_ref):
    comps, nx, ny, nz = field_ref.shape
    region = lax.axis_index("region")
    block = lax.axis_index("blk")
    no_xlo = region == 0
    no_xhi = region == lax.axis_size("region") - 1
    no_ylo = block == 0
    no_yhi = block == lax.axis_size("blk") - 1
    for c in range(comps):
        padded[c, 2 : 2 + nx, 8 : 8 + ny, :] = field_ref[c]
        padded[c, 0:2, 8 : 8 + ny, :] = jnp.where(no_xlo, 0.0, xlo_ref[c])
        padded[c, 2 + nx : 4 + nx, 8 : 8 + ny, :] = jnp.where(no_xhi, 0.0, xhi_ref[c])
        padded[c, 2 : 2 + nx, 6:8, :] = jnp.where(no_ylo, 0.0, ylo_ref[c])
        padded[c, 2 : 2 + nx, 8 + ny : 10 + ny, :] = jnp.where(no_yhi, 0.0, yhi_ref[c])


def stencil(padded, viscosity_ref, emit):
    comps = padded.shape[0]
    nx, ny, nz = viscosity_ref.shape
    lane = lax.broadcasted_iota(jnp.int32, (8, nz), 1)

    def plane(x, carry):
        for tile in range(ny // 8):
            y = 8 + 8 * tile
            centers = [padded[c, x + 2, y : y + 8, :] for c in range(comps)]
            scaled = [value * (1.0 / 12.0) for value in centers]
            visc = viscosity_ref[x, 8 * tile : 8 * tile + 8, :] * (1.0 / 12.0)
            for c in range(comps):
                here = centers[c]
                near = None
                for axis in range(3):
                    if axis == 0:
                        a1 = padded[c, x + 3, y : y + 8, :]
                        b1 = padded[c, x + 1, y : y + 8, :]
                        a2 = padded[c, x + 4, y : y + 8, :]
                        b2 = padded[c, x, y : y + 8, :]
                    elif axis == 1:
                        a1 = padded[c, x + 2, y + 1 : y + 9, :]
                        b1 = padded[c, x + 2, y - 1 : y + 7, :]
                        a2 = padded[c, x + 2, y + 2 : y + 10, :]
                        b2 = padded[c, x + 2, y - 2 : y + 6, :]
                    else:
                        a1 = jnp.where(lane < nz - 1, pltpu.roll(here, nz - 1, 1), 0.0)
                        b1 = jnp.where(lane >= 1, pltpu.roll(here, 1, 1), 0.0)
                        a2 = jnp.where(lane < nz - 2, pltpu.roll(here, nz - 2, 1), 0.0)
                        b2 = jnp.where(lane >= 2, pltpu.roll(here, 2, 1), 0.0)
                    slope = 8.0 * (a1 - b1) - (a2 - b2)
                    if near is None:
                        near = a1 + b1
                        far = a2 + b2
                        advect = scaled[axis] * slope
                    else:
                        near = near + (a1 + b1)
                        far = far + (a2 + b2)
                        advect = advect + scaled[axis] * slope
                spread = 16.0 * near - far - 90.0 * here
                emit(c, x, 8 * tile, here, visc * spread - advect)
        return carry

    lax.fori_loop(0, nx, plane, 0)


def sample_at(field_ref, cells, split, picked):
    comps, nx, ny, nz = field_ref.shape
    points = cells.shape[1]
    rows = nx * ny
    for c in range(comps):
        values = field_ref[c].reshape(rows, nz)
        for index, part in enumerate(pieces_of(values, PIECES)):
            split[c * rows : (c + 1) * rows, index * nz : (index + 1) * nz] = part
    lane_cell = cells & (nz - 1)
    row_cell = cells // nz
    width = 256
    sums = [[] for _ in range(comps)]
    for start in range(0, points, width):
        lanes = slice(start, start + width)
        hot = jnp.where(row_iota((nz, width)) == lane_cell[:, lanes], 1.0, 0.0).astype(BF16)
        hots = jnp.concatenate([hot] * PIECES, axis=0)
        picked[...] = jnp.dot(split[...], hots, preferred_element_type=F32)
        mask = row_iota((rows, width)) == row_cell[:, lanes]
        for c in range(comps):
            block = picked[c * rows : (c + 1) * rows, :]
            sums[c].append(jnp.sum(jnp.where(mask, block, 0.0), axis=0, keepdims=True))
    return [jnp.concatenate(parts, axis=1) for parts in sums]


def scatter_sum(stresses, cells, live, shape):
    comps, nx, ny, nz = shape
    points = cells.shape[1]
    rows = nx * ny
    lane_cell = cells & (nz - 1)
    row_cell = cells // nz
    hot = jnp.where(row_iota((rows, points)) == row_cell, 1.0, 0.0).astype(BF16)
    match = (row_iota((nz, points)) == lane_cell) & live
    total = None
    split = [pieces_of(value, PIECES) for value in stresses]
    for index in range(PIECES):
        spread = jnp.concatenate(
            [
                jnp.where(match, split[c][index].astype(F32), 0.0).astype(BF16)
                for c in range(comps)
            ],
            axis=0,
        )
        part = lax.dot_general(
            hot, spread, (((1,), (1,)), ((), ())), preferred_element_type=F32
        )
        total = part if total is None else total + part
    return total


def wall_solve(samples, distance, normals):
    points = distance.shape[1]
    normal_part = sum(s * n for s, n in zip(samples, normals))
    tangent = [s - normal_part * n for s, n in zip(samples, normals)]
    speed = jnp.maximum(jnp.sqrt(sum(t * t for t in tangent)), SPEED_FLOOR)
    target = jnp.log(speed)
    log_speed = target - jnp.log(jnp.full_like(target, GUESS_RATIO))
    index = row_iota((ETAS, points)).astype(F32)
    top = ETAS - 1.0
    eta = (index / top) * (index / top)
    upper = jnp.minimum(index + 1.0, top) / top
    lower = jnp.maximum(index - 1.0, 0.0) / top
    weight = 0.5 * (upper * upper - lower * lower)
    for _ in range(NEWTON):
        pace = jnp.exp(log_speed)
        height = eta * (distance * pace)
        decay = height * (1.0 / (NU_WALL * DAMPING))
        fade = jnp.exp(-decay)
        damp = 1.0 - fade
        mixing = KAPPA * height * damp
        share = weight / (NU_WALL + mixing * damp)
        growth = mixing * (damp + 2.0 * decay * fade)
        total = jnp.sum(share, axis=0, keepdims=True)
        change = jnp.sum(share * growth / (NU_WALL + mixing * damp), axis=0, keepdims=True)
        value = jnp.log(distance * pace * pace * total) - target
        log_speed = log_speed - value / (2.0 - change / total)
    stress = jnp.exp(2.0 * log_speed)
    factor = -stress / speed
    return [factor * t for t in tangent], 2.0 * log_speed


def first_kernel(
    velocity_ref, viscosity_ref, xlo_ref, xhi_ref, ylo_ref, yhi_ref, match_ref, dest_ref,
    base_ref, samples_ref, rank_ref, padded, split, picked,
):
    points = match_ref.shape[0] * match_ref.shape[1]
    cells = as_row(match_ref[...])
    samples = sample_at(velocity_ref, cells, split, picked)
    for c in range(3):
        samples_ref[c : c + 1, :] = samples[c]
    owners = as_row(dest_ref[...])
    devices = lax.axis_size("region") * lax.axis_size("blk")
    width = 128
    before = jnp.where(
        row_iota((width, width)) < lax.broadcasted_iota(jnp.int32, (width, width), 1), 1.0, 0.0
    )
    table = jnp.concatenate([before, jnp.ones((width, width), F32)], axis=0).astype(BF16)
    earlier = jnp.zeros((devices, width), F32)
    for start in range(0, points, width):
        hot = jnp.where(row_iota((devices, width)) == owners[:, start : start + width], 1.0, 0.0)
        both = jnp.concatenate([hot, earlier], axis=1).astype(BF16)
        running = jnp.dot(both, table, preferred_element_type=F32)
        rank_ref[0:1, start : start + width] = jnp.sum(hot * running, axis=0, keepdims=True)
        earlier = earlier + hot
    fill_padded(padded, velocity_ref, xlo_ref, xhi_ref, ylo_ref, yhi_ref)

    def emit(c, x, y, here, rate):
        base_ref[c, x, y : y + 8, :] = here + TIME_STEP * rate

    stencil(padded, viscosity_ref, emit)


def live_row(count_ref, points):
    return lax.broadcasted_iota(jnp.int32, (1, points), 1) < count_ref[0]


def stress_kernel(
    count_ref, arrived_ref, dest_ref, wall_ref, rank_ref, samples_ref, base_ref,
    first_ref, xlow_ref, xhigh_ref, ylow_ref, yhigh_ref, geometry_ref,
):
    comps, nx, ny, nz = base_ref.shape
    devices, fields = arrived_ref.shape
    capacity = fields // 4
    points = wall_ref.shape[0] * wall_ref.shape[1]
    owners = as_row(dest_ref[...])
    hot = jnp.where(row_iota((devices, points)) == owners, 1.0, 0.0).astype(BF16)
    table = None
    for part in pieces_of(arrived_ref[...], 3):
        term = lax.dot_general(
            part, hot, (((0,), (0,)), ((), ())), preferred_element_type=F32
        )
        table = term if table is None else table + term
    rank = rank_ref[0:1, :].astype(jnp.int32)
    mask = row_iota((capacity, points)) == rank
    rows = [
        jnp.sum(
            jnp.where(mask, table[k * capacity : (k + 1) * capacity, :], 0.0),
            axis=0, keepdims=True,
        )
        for k in range(4)
    ]
    distance = rows[0]
    length = jnp.sqrt(rows[1] * rows[1] + rows[2] * rows[2] + rows[3] * rows[3])
    normals = [row / length for row in rows[1:]]
    geometry_ref[0:1, :] = distance
    for k in range(3):
        geometry_ref[k + 1 : k + 2, :] = normals[k]
    samples = [samples_ref[c : c + 1, :] for c in range(3)]
    stress, _ = wall_solve(samples, distance, normals)
    live = live_row(count_ref, points)
    stress = [jnp.where(live, value, 0.0) for value in stress]
    force = scatter_sum(stress, as_row(wall_ref[...]), live, base_ref.shape)
    for c in range(comps):
        block = force[:, c * nz : (c + 1) * nz] * (TIME_STEP / WALL_DY)
        first_ref[c] = base_ref[c] + block.reshape(nx, ny, nz)
        xlow_ref[c] = first_ref[c, 0:2]
        xhigh_ref[c] = first_ref[c, nx - 2 : nx]
        ylow_ref[c] = first_ref[c, :, 0:2, :]
        yhigh_ref[c] = first_ref[c, :, ny - 2 : ny, :]


def second_kernel(
    count_ref, first_ref, match_ref, wall_ref, geometry_ref, force_ref, log_ref, split, picked,
):
    comps, nx, ny, nz = first_ref.shape
    points = wall_ref.shape[0] * wall_ref.shape[1]
    samples = sample_at(first_ref, as_row(match_ref[...]), split, picked)
    distance = geometry_ref[0:1, :]
    normals = [geometry_ref[k : k + 1, :] for k in range(1, 4)]
    stress, log_stress = wall_solve(samples, distance, normals)
    live = live_row(count_ref, points)
    log_stress = jnp.where(live, log_stress, 0.0)
    for i in range(log_ref.shape[0]):
        log_ref[i : i + 1, :] = log_stress[:, i * 128 : (i + 1) * 128]
    stress = [jnp.where(live, value, 0.0) for value in stress]
    force = scatter_sum(stress, as_row(wall_ref[...]), live, first_ref.shape)
    for c in range(comps):
        block = force[:, c * nz : (c + 1) * nz] * (0.5 * TIME_STEP / WALL_DY)
        force_ref[c] = block.reshape(nx, ny, nz)


def last_kernel(
    velocity_ref, viscosity_ref, first_ref, force_ref, xlo_ref, xhi_ref, ylo_ref, yhi_ref,
    advanced_ref, padded,
):
    fill_padded(padded, first_ref, xlo_ref, xhi_ref, ylo_ref, yhi_ref)

    def emit(c, x, y, here, rate):
        rows = slice(y, y + 8)
        mean = 0.5 * (velocity_ref[c, x, rows, :] + here)
        advanced_ref[c, x, rows, :] = mean + (
            0.5 * TIME_STEP * rate + force_ref[c, x, rows, :]
        )

    stencil(padded, viscosity_ref, emit)


def ring(axis, step):
    count = lax.axis_size(axis)
    return [(i, (i + step) % count) for i in range(count)]


def shift(block, axis, step):
    return lax.ppermute(block, axis, ring(axis, step))


def exchange(xlow, xhigh, ylow, yhigh):
    return (
        shift(xhigh, "region", 1),
        shift(xlow, "region", -1),
        shift(yhigh, "blk", 1),
        shift(ylow, "blk", -1),
    )


def local(velocity, viscosity, match_cell, wall_cell, match_dest, match_count, wall_geom):
    devices = lax.axis_size("region") * lax.axis_size("blk")
    capacity = wall_geom.shape[1] // devices
    points = match_cell.shape[0]
    comps, nx, ny, nz = velocity.shape
    field = jax.ShapeDtypeStruct(velocity.shape, F32)
    xface = jax.ShapeDtypeStruct((comps, 2, ny, nz), F32)
    yface = jax.ShapeDtypeStruct((comps, nx, 2, nz), F32)
    rowed = jax.ShapeDtypeStruct((4, points), F32)
    square = (points // 128, 128)
    match = match_cell.reshape(square)
    wall = wall_cell.reshape(square)
    dest = match_dest.reshape(square)
    vmem = pl.BlockSpec(memory_space=pltpu.VMEM)
    smem = pl.BlockSpec(memory_space=pltpu.SMEM)
    padded = pltpu.VMEM((comps, nx + 4, ny + 16, nz), F32)
    split = pltpu.VMEM((comps * nx * ny, PIECES * nz), BF16)
    picked = pltpu.VMEM((comps * nx * ny, 256), F32)

    outgoing = wall_geom.reshape(4, devices, capacity).transpose(1, 0, 2).reshape(devices, -1)
    arrived = lax.all_to_all(
        outgoing, ("region", "blk"), split_axis=0, concat_axis=0, tiled=True
    )
    halos = exchange(
        velocity[:, 0:2], velocity[:, nx - 2 :], velocity[:, :, 0:2], velocity[:, :, ny - 2 :]
    )
    base, samples, rank = pl.pallas_call(
        first_kernel,
        out_shape=(field, rowed, jax.ShapeDtypeStruct((1, points), F32)),
        in_specs=[vmem] * 8,
        out_specs=(vmem,) * 3,
        scratch_shapes=[padded, split, picked],
        name="first",
    )(velocity, viscosity, *halos, match, dest)
    first, *faces, geometry = pl.pallas_call(
        stress_kernel,
        out_shape=(field, xface, xface, yface, yface, rowed),
        in_specs=[smem] + [vmem] * 6,
        out_specs=(vmem,) * 6,
        name="stress",
    )(match_count, arrived, dest, wall, rank, samples, base)
    halos = exchange(*faces)
    force, log_stress = pl.pallas_call(
        second_kernel,
        out_shape=(field, jax.ShapeDtypeStruct(square, F32)),
        in_specs=[smem] + [vmem] * 4,
        out_specs=(vmem,) * 2,
        scratch_shapes=[split, picked],
        name="second",
    )(match_count, first, match, wall, geometry)
    advanced = pl.pallas_call(
        last_kernel,
        out_shape=field,
        in_specs=[vmem] * 8,
        out_specs=vmem,
        scratch_shapes=[padded],
        name="last",
    )(velocity, viscosity, first, force, *halos)
    return (advanced, log_stress.reshape(points))


def solution(mesh):
    placed = (
        P(None, "region", "blk", None),
        P("region", "blk", None),
        P(("region", "blk")),
        P(("region", "blk")),
        P(("region", "blk"), None),
        P(("region", "blk")),
        P(None, ("region", "blk")),
    )
    return jax.shard_map(
        local,
        mesh=mesh,
        in_specs=placed,
        out_specs=(P(None, "region", "blk", None), P(("region", "blk"))),
        check_vma=False,
    )
```

profile of v0, /device:TPU:0, one launch (start us, length us, event | category | flops | bytes accessed | tf_op | source)
XLA Modules:
  0.0 68.0 jit_solution(13832783384198932193)
XLA Ops:
  0.6 1.1 %fusion.1 = (f32[3,2,32,256]{3,2,1,0:T(8,128)S(1)}, f32[3,2,32,256]{3,2,1,0:T(8,128)S(1)}) fusion(f32[3,16,32,256]{3,2,1,0:T(8,128)} %velocity_ref.3), kind=kLoop, calls=%fused_computation.1 | loop fusion | bytes 786432 | tf_op jit(solution)/shard_map/slice | solution.py:343
  1.7 2.3 %collective-permute-start.1 = (f32[3,2,32,256]{3,2,1,0:T(8,128)S(1)}, f32[3,2,32,256]{3,2,1,0:T(8,128)S(1)}, u32[]{:S(2)}, u32[]{:S(2)}) collective-permute-start(f32[3,2,32,256]{3,2,1,0:T(8,128)S(1)} %get-tuple-element.26), channel_id=1, source_target_pairs={{0,112},{16,0},{32,16},{48,32},{64,48},{80,64},{96,80},{112,96},{1... | collective-permute-start | bytes 589832 | tf_op jit(solution)/shard_map/ppermute | solution.py:307
  4.0 1.2 %fusion = (f32[3,16,2,256]{3,2,1,0:T(2,128)S(1)}, f32[3,16,2,256]{3,2,1,0:T(2,128)S(1)}) fusion(f32[3,16,32,256]{3,2,1,0:T(8,128)} %velocity_ref.3), kind=kLoop, calls=%fused_computation | loop fusion | bytes 393216 | tf_op jit(solution)/shard_map/slice | solution.py:343
  5.2 6.6 %collective-permute-start.3 = (f32[3,16,2,256]{3,2,1,0:T(2,128)S(1)}, f32[3,16,2,256]{3,2,1,0:T(2,128)S(1)}, u32[]{:S(2)}, u32[]{:S(2)}) collective-permute-start(f32[3,16,2,256]{3,2,1,0:T(2,128)S(1)} %get-tuple-element.24), channel_id=1, source_target_pairs={{0,15},{1,0},{2,1},{3,2},{4,3},{5,4},{6,5},{7,6},{8,7},{9,8},{10,9... | collective-permute-start | bytes 294920 | tf_op jit(solution)/shard_map/ppermute | solution.py:307
  11.8 0.9 %reshape.23 = f32[4,128,16]{2,1,0:T(8,128)S(1)} reshape(f32[4,2048]{1,0:T(4,128)} %param.13) | data formatting | bytes 65536 | tf_op jit(solution)/shard_map/reshape | solution.py:338
  12.7 0.1 copy.12
  12.8 0.7 %copy.13 = f32[128,1,64]{2,1,0:T(1,128)} copy(f32[128,1,64]{0,2,1:T(8,128)S(1)} %bitcast.9) | data formatting | bytes 65536 | tf_op jit(solution)/shard_map/all_to_all | solution.py:339
  13.5 9.1 %all-to-all-start = ((f32[128,1,64]{2,1,0:T(1,128)}), f32[128,1,64]{2,1,0:T(1,128)S(1)}, u32[]{:S(2)}, u32[]{:S(2)}) async-start(f32[128,1,64]{2,1,0:T(1,128)} %copy.13), calls=%async_computation | async-start | bytes 131072 | tf_op jit(solution)/shard_map/all_to_all | solution.py:339
  23.3 0.6 copy-done.7
  23.9 0.0 copy-done.8
  23.9 0.1 copy-done.1
  24.0 0.1 copy-done.2
  24.1 10.0 %first.1 = (f32[3,16,32,256]{3,2,1,0:T(8,128)}, f32[4,1024]{1,0:T(4,128)}, f32[1,1024]{1,0:T(1,128)}) custom-call(f32[3,16,32,256]{3,2,1,0:T(8,128)} %velocity_ref.3, f32[16,32,256]{2,1,0:T(8,128)} %viscosity_ref.3, f32[3,2,32,256]{3,2,1,0:T(8,128)} %copy-done.2, f32[3,2,32,256]{3,2,1,0:T(8,128)} %copy-done.1, f32[3,16,2,256]{3,2,1,0:T(2,128)} %copy-done.8, ...), custom_call_target="tpu_custom_call" | custom-call | tf_op jit(solution)/shard_map/first/pallas_call | solution.py:345
  34.1 0.6 copy-done
  34.7 6.3 %stress.1 = (f32[3,16,32,256]{3,2,1,0:T(8,128)}, f32[3,2,32,256]{3,2,1,0:T(8,128)}, f32[3,2,32,256]{3,2,1,0:T(8,128)}, f32[3,16,2,256]{3,2,1,0:T(2,128)}, f32[3,16,2,256]{3,2,1,0:T(2,128)}, /*index=5*/f32[4,1024]{1,0:T(4,128)}) custom-call(s32[1]{0:T(128)S(6)} %copy.14.count_ref, f32[128,64]{1,0:T(8,128)} %bitcast.8, s32[8,128]{1,0:T(8,128)} %bitcast.11, ...), custom_call_target="tpu_custom_call" | custom-call | tf_op jit(solution)/shard_map/stress/pallas_call | solution.py:353
  41.0 3.0 %collective-permute-start.5 = (f32[3,2,32,256]{3,2,1,0:T(8,128)}, f32[3,2,32,256]{3,2,1,0:T(8,128)S(1)}, u32[]{:S(2)}, u32[]{:S(2)}) collective-permute-start(f32[3,2,32,256]{3,2,1,0:T(8,128)} %get-tuple-element.20), channel_id=1, source_target_pairs={{0,112},{16,0},{32,16},{48,32},{64,48},{80,64},{96,80},{112,96},{1... | collective-permute-start | bytes 589832 | tf_op jit(solution)/shard_map/ppermute | solution.py:307
  44.0 1.1 %collective-permute-start.6 = (f32[3,16,2,256]{3,2,1,0:T(2,128)}, f32[3,16,2,256]{3,2,1,0:T(2,128)S(1)}, u32[]{:S(2)}, u32[]{:S(2)}) collective-permute-start(f32[3,16,2,256]{3,2,1,0:T(2,128)} %get-tuple-element.21), channel_id=1, source_target_pairs={{0,1},{1,2},{2,3},{3,4},{4,5},{5,6},{6,7},{7,8},{8,9},{9,10},{10,1... | collective-permute-start | bytes 294920 | tf_op jit(solution)/shard_map/ppermute | solution.py:307
  45.1 4.3 %collective-permute-start.7 = (f32[3,16,2,256]{3,2,1,0:T(2,128)}, f32[3,16,2,256]{3,2,1,0:T(2,128)S(1)}, u32[]{:S(2)}, u32[]{:S(2)}) collective-permute-start(f32[3,16,2,256]{3,2,1,0:T(2,128)} %get-tuple-element.22), channel_id=1, source_target_pairs={{0,15},{1,0},{2,1},{3,2},{4,3},{5,4},{6,5},{7,6},{8,7},{9,8},{10,9... | collective-permute-start | bytes 294920 | tf_op jit(solution)/shard_map/ppermute | solution.py:307
  49.3 10.0 %second.1 = (f32[3,16,32,256]{3,2,1,0:T(8,128)}, f32[8,128]{1,0:T(8,128)}) custom-call(s32[1]{0:T(128)S(6)} %copy.14.count_ref, f32[3,16,32,256]{3,2,1,0:T(8,128)} %get-tuple-element.16.first_ref, s32[8,128]{1,0:T(8,128)} %bitcast.15, s32[8,128]{1,0:T(8,128)} %bitcast.13, f32[4,1024]{1,0:T(4,128)} %get-tuple-element.17.geometry_ref), custom_call_target="tpu_custom_call" | custom-call | tf_op jit(solution)/shard_map/second/pallas_call | solution.py:361
  59.5 0.6 copy-done.5
  60.0 0.0 copy-done.6
  60.1 0.1 copy-done.3
  60.1 0.1 copy-done.4
  60.2 7.8 %last.1 = f32[3,16,32,256]{3,2,1,0:T(8,128)} custom-call(f32[3,16,32,256]{3,2,1,0:T(8,128)} %velocity_ref.3, f32[16,32,256]{2,1,0:T(8,128)} %viscosity_ref.3, f32[3,16,32,256]{3,2,1,0:T(8,128)} %get-tuple-element.16.first_ref, f32[3,16,32,256]{3,2,1,0:T(8,128)} %get-tuple-element.18.force_ref, f32[3,2,32,256]{3,2,1,0:T(8,128)} %copy-done.3, ...), custom_call_target="tpu_custom_call" | custom-call | tf_op jit(solution)/shard_map/last/pallas_call | solution.py:369
  (21 shorter events, 0.0 us)
Async XLA Ops:
  1.7 21.6 %collective-permute-start.1 = (f32[3,2,32,256]{3,2,1,0:T(8,128)S(1)}, f32[3,2,32,256]{3,2,1,0:T(8,128)S(1)}, u32[]{:S(2)}, u32[]{:S(2)}) collective-permute-start(f32[3,2,32,256]{3,2,1,0:T(8,128)S(1)} %get-tuple-element.26), channel_id=1, source_target_pairs={{0,112},{16,0},{32,16},{48,32},{64,48},{80,64},{96,80},{112,96},{1... | collective-permute-start | bytes 589832 | tf_op jit(solution)/shard_map/ppermute | solution.py:307
  4.0 19.3 %collective-permute-start = (f32[3,2,32,256]{3,2,1,0:T(8,128)S(1)}, f32[3,2,32,256]{3,2,1,0:T(8,128)S(1)}, u32[]{:S(2)}, u32[]{:S(2)}) collective-permute-start(f32[3,2,32,256]{3,2,1,0:T(8,128)S(1)} %get-tuple-element.27), channel_id=1, source_target_pairs={{0,16},{16,32},{32,48},{48,64},{64,80},{80,96},{96,112},{112,0},{1... | collective-permute-start | bytes 589832 | tf_op jit(solution)/shard_map/ppermute | solution.py:307
  5.2 18.1 %collective-permute-start.3 = (f32[3,16,2,256]{3,2,1,0:T(2,128)S(1)}, f32[3,16,2,256]{3,2,1,0:T(2,128)S(1)}, u32[]{:S(2)}, u32[]{:S(2)}) collective-permute-start(f32[3,16,2,256]{3,2,1,0:T(2,128)S(1)} %get-tuple-element.24), channel_id=1, source_target_pairs={{0,15},{1,0},{2,1},{3,2},{4,3},{5,4},{6,5},{7,6},{8,7},{9,8},{10,9... | collective-permute-start | bytes 294920 | tf_op jit(solution)/shard_map/ppermute | solution.py:307
  11.8 11.5 %collective-permute-start.2 = (f32[3,16,2,256]{3,2,1,0:T(2,128)S(1)}, f32[3,16,2,256]{3,2,1,0:T(2,128)S(1)}, u32[]{:S(2)}, u32[]{:S(2)}) collective-permute-start(f32[3,16,2,256]{3,2,1,0:T(2,128)S(1)} %get-tuple-element.25), channel_id=1, source_target_pairs={{0,1},{1,2},{2,3},{3,4},{4,5},{5,6},{6,7},{7,8},{8,9},{9,10},{10,1... | collective-permute-start | bytes 294920 | tf_op jit(solution)/shard_map/ppermute | solution.py:307
  13.5 20.6 %all-to-all-start = ((f32[128,1,64]{2,1,0:T(1,128)}), f32[128,1,64]{2,1,0:T(1,128)S(1)}, u32[]{:S(2)}, u32[]{:S(2)}) async-start(f32[128,1,64]{2,1,0:T(1,128)} %copy.13), calls=%async_computation | async-start | bytes 131072 | tf_op jit(solution)/shard_map/all_to_all | solution.py:339
  23.3 0.6 copy-start.7
  23.3 0.7 copy-start.8
  23.3 0.7 %copy-start.1 = (f32[3,2,32,256]{3,2,1,0:T(8,128)}, f32[3,2,32,256]{3,2,1,0:T(8,128)S(1)}, u32[]{:S(2)}) copy-start(f32[3,2,32,256]{3,2,1,0:T(8,128)S(1)} %collective-permute-done.1.xhi_ref) | copy-start | bytes 589828
  23.3 0.8 %copy-start.2 = (f32[3,2,32,256]{3,2,1,0:T(8,128)}, f32[3,2,32,256]{3,2,1,0:T(8,128)S(1)}, u32[]{:S(2)}) copy-start(f32[3,2,32,256]{3,2,1,0:T(8,128)S(1)} %collective-permute-done.xlo_ref) | copy-start | bytes 589828
  34.1 0.6 copy-start
  41.0 18.4 %collective-permute-start.4 = (f32[3,2,32,256]{3,2,1,0:T(8,128)}, f32[3,2,32,256]{3,2,1,0:T(8,128)S(1)}, u32[]{:S(2)}, u32[]{:S(2)}) collective-permute-start(f32[3,2,32,256]{3,2,1,0:T(8,128)} %get-tuple-element.19), channel_id=1, source_target_pairs={{0,16},{16,32},{32,48},{48,64},{64,80},{80,96},{96,112},{112,0},{1... | collective-permute-start | bytes 589832 | tf_op jit(solution)/shard_map/ppermute | solution.py:307
  41.0 18.4 %collective-permute-start.5 = (f32[3,2,32,256]{3,2,1,0:T(8,128)}, f32[3,2,32,256]{3,2,1,0:T(8,128)S(1)}, u32[]{:S(2)}, u32[]{:S(2)}) collective-permute-start(f32[3,2,32,256]{3,2,1,0:T(8,128)} %get-tuple-element.20), channel_id=1, source_target_pairs={{0,112},{16,0},{32,16},{48,32},{64,48},{80,64},{96,80},{112,96},{1... | collective-permute-start | bytes 589832 | tf_op jit(solution)/shard_map/ppermute | solution.py:307
  44.0 15.4 %collective-permute-start.6 = (f32[3,16,2,256]{3,2,1,0:T(2,128)}, f32[3,16,2,256]{3,2,1,0:T(2,128)S(1)}, u32[]{:S(2)}, u32[]{:S(2)}) collective-permute-start(f32[3,16,2,256]{3,2,1,0:T(2,128)} %get-tuple-element.21), channel_id=1, source_target_pairs={{0,1},{1,2},{2,3},{3,4},{4,5},{5,6},{6,7},{7,8},{8,9},{9,10},{10,1... | collective-permute-start | bytes 294920 | tf_op jit(solution)/shard_map/ppermute | solution.py:307
  45.1 14.3 %collective-permute-start.7 = (f32[3,16,2,256]{3,2,1,0:T(2,128)}, f32[3,16,2,256]{3,2,1,0:T(2,128)S(1)}, u32[]{:S(2)}, u32[]{:S(2)}) collective-permute-start(f32[3,16,2,256]{3,2,1,0:T(2,128)} %get-tuple-element.22), channel_id=1, source_target_pairs={{0,15},{1,0},{2,1},{3,2},{4,3},{5,4},{6,5},{7,6},{8,7},{9,8},{10,9... | collective-permute-start | bytes 294920 | tf_op jit(solution)/shard_map/ppermute | solution.py:307
  59.4 0.6 copy-start.5
  59.4 0.7 copy-start.6
  59.4 0.7 %copy-start.3 = (f32[3,2,32,256]{3,2,1,0:T(8,128)}, f32[3,2,32,256]{3,2,1,0:T(8,128)S(1)}, u32[]{:S(2)}) copy-start(f32[3,2,32,256]{3,2,1,0:T(8,128)S(1)} %collective-permute-done.4.xlo_ref) | copy-start | bytes 589828
  59.4 0.8 %copy-start.4 = (f32[3,2,32,256]{3,2,1,0:T(8,128)}, f32[3,2,32,256]{3,2,1,0:T(8,128)S(1)}, u32[]{:S(2)}) copy-start(f32[3,2,32,256]{3,2,1,0:T(8,128)S(1)} %collective-permute-done.5.xhi_ref) | copy-start | bytes 589828
where the time goes:
time: 68.4 us; the launch traced here: 68 us
  Pallas kernels  34.2 us (50%)
  starting transfers between devices  26.3 us (38%)
  local copies, waits for them, and re-layouts  6.1 us (9%)
  between operations  1.43 us (2%)
    ppermute x8, starting transfers between devices, shift(): return lax.ppermute(block, axis, ring(axis, step))  17.2 us
    pallas_call x1, Pallas kernels, local(): pl.pallas_call(second_kernel, out_shape=(field, jax.ShapeDtypeStruct(squa...  10 us
    pallas_call x1, Pallas kernels, local(): pl.pallas_call(first_kernel, out_shape=(field, rowed, jax.ShapeDtypeStruc...  9.96 us
    all_to_all x1, starting transfers between devices, local(): lax.all_to_all(outgoing, ('region', 'blk'), split_axis=0, concat_axis=0,...  9.1 us
    pallas_call x1, Pallas kernels, local(): pl.pallas_call(last_kernel, out_shape=field, in_specs=[vmem] * 8, out_spe...  7.84 us
    pallas_call x1, Pallas kernels, local(): pl.pallas_call(stress_kernel, out_shape=(field, xface, xface, yface, yfac...  6.35 us
    unnamed x18, local copies, waits for them, and re-layouts  2.13 us
  transfers between devices with their start and end apart: 9, of which 0 were waited for; matrix products, arithmetic and copies ran while one was open for 4% of the time, Pallas kernels for 29%

commit v1 on v0

--- a/solution.py
+++ b/solution.py
@@ -15,7 +15,7 @@
 SPEED_FLOOR = 0.5
 GUESS_RATIO = 14.0
 ETAS = 32
-PIECES = 3
+PIECES = 2
 F32 = jnp.float32
 BF16 = jnp.bfloat16
 
@@ -40,63 +40,87 @@
     return lax.broadcasted_iota(jnp.int32, shape, 0)
 
 
-def fill_padded(padded, field_ref, xlo_ref, xhi_ref, ylo_ref, yhi_ref):
+def even_side(axis):
+    return lax.axis_index(axis) % 2 == 0
+
+
+def at_end(axis):
+    place = lax.axis_index(axis)
+    return (place == 0) | (place == lax.axis_size(axis) - 1)
+
+
+def fill_padded(padded, field_ref, xa_ref, xb_ref, ya_ref, yb_ref):
     comps, nx, ny, nz = field_ref.shape
-    region = lax.axis_index("region")
-    block = lax.axis_index("blk")
-    no_xlo = region == 0
-    no_xhi = region == lax.axis_size("region") - 1
-    no_ylo = block == 0
-    no_yhi = block == lax.axis_size("blk") - 1
+    even_x, even_y = even_side("region"), even_side("blk")
+    end_x, end_y = at_end("region"), at_end("blk")
+    spot_a = jnp.where(even_x, nx + 2, 0)
+    spot_b = nx + 2 - spot_a
     for c in range(comps):
-        padded[c, 2 : 2 + nx, 8 : 8 + ny, :] = field_ref[c]
-        padded[c, 0:2, 8 : 8 + ny, :] = jnp.where(no_xlo, 0.0, xlo_ref[c])
-        padded[c, 2 + nx : 4 + nx, 8 : 8 + ny, :] = jnp.where(no_xhi, 0.0, xhi_ref[c])
-        padded[c, 2 : 2 + nx, 6:8, :] = jnp.where(no_ylo, 0.0, ylo_ref[c])
-        padded[c, 2 : 2 + nx, 8 + ny : 10 + ny, :] = jnp.where(no_yhi, 0.0, yhi_ref[c])
-
-
-def stencil(padded, viscosity_ref, emit):
-    comps = padded.shape[0]
-    nx, ny, nz = viscosity_ref.shape
-    lane = lax.broadcasted_iota(jnp.int32, (8, nz), 1)
+        near_x = xa_ref[c]
+        far_x = jnp.where(end_x, 0.0, xb_ref[c])
+        near_y = ya_ref[c]
+        far_y = jnp.where(end_y, 0.0, yb_ref[c])
+        low_y = jnp.where(even_y, far_y, near_y)
+        high_y = jnp.where(even_y, near_y, far_y)
+        for h in range(nz // 128):
+            lanes = slice(128 * h, 128 * h + 128)
+            padded[c, h, 2 : 2 + nx, 8 : 8 + ny, :] = field_ref[c, :, :, lanes]
+            padded[c, h, pl.ds(spot_a, 2), 8 : 8 + ny, :] = near_x[:, :, lanes]
+            padded[c, h, pl.ds(spot_b, 2), 8 : 8 + ny, :] = far_x[:, :, lanes]
+            padded[c, h, 2 : 2 + nx, 6:8, :] = low_y[:, :, lanes]
+            padded[c, h, 2 : 2 + nx, 8 + ny : 10 + ny, :] = high_y[:, :, lanes]
+
+
+def stencil(padded, viscosity_ref, step, emit):
+    comps, halves = padded.shape[:2]
+    nx, ny, _ = viscosity_ref.shape
+    lane = lax.broadcasted_iota(jnp.int32, (8, 128), 1)
+    top = [lane < 127, lane < 126]
+    bottom = [lane >= 1, lane >= 2]
+    scale = step / 12.0
 
     def plane(x, carry):
         for tile in range(ny // 8):
             y = 8 + 8 * tile
-            centers = [padded[c, x + 2, y : y + 8, :] for c in range(comps)]
-            scaled = [value * (1.0 / 12.0) for value in centers]
-            visc = viscosity_ref[x, 8 * tile : 8 * tile + 8, :] * (1.0 / 12.0)
-            for c in range(comps):
-                here = centers[c]
-                near = None
-                for axis in range(3):
-                    if axis == 0:
-                        a1 = padded[c, x + 3, y : y + 8, :]
-                        b1 = padded[c, x + 1, y : y + 8, :]
-                        a2 = padded[c, x + 4, y : y + 8, :]
-                        b2 = padded[c, x, y : y + 8, :]
-                    elif axis == 1:
-                        a1 = padded[c, x + 2, y + 1 : y + 9, :]
-                        b1 = padded[c, x + 2, y - 1 : y + 7, :]
-                        a2 = padded[c, x + 2, y + 2 : y + 10, :]
-                        b2 = padded[c, x + 2, y - 2 : y + 6, :]
-                    else:
-                        a1 = jnp.where(lane < nz - 1, pltpu.roll(here, nz - 1, 1), 0.0)
-                        b1 = jnp.where(lane >= 1, pltpu.roll(here, 1, 1), 0.0)
-                        a2 = jnp.where(lane < nz - 2, pltpu.roll(here, nz - 2, 1), 0.0)
-                        b2 = jnp.where(lane >= 2, pltpu.roll(here, 2, 1), 0.0)
-                    slope = 8.0 * (a1 - b1) - (a2 - b2)
-                    if near is None:
-                        near = a1 + b1
-                        far = a2 + b2
-                        advect = scaled[axis] * slope
-                    else:
-                        near = near + (a1 + b1)
-                        far = far + (a2 + b2)
-                        advect = advect + scaled[axis] * slope
-                spread = 16.0 * near - far - 90.0 * here
-                emit(c, x, 8 * tile, here, visc * spread - advect)
+            here = [
+                [padded[c, h, x + 2, y : y + 8, :] for h in range(halves)] for c in range(comps)
+            ]
+            for h in range(halves):
+                lanes = slice(128 * h, 128 * h + 128)
+                visc = viscosity_ref[x, 8 * tile : 8 * tile + 8, lanes] * scale
+                speed = [here[c][h] * scale for c in range(comps)]
+                for c in range(comps):
+
+                    def along_z(shift):
+                        count = abs(shift)
+                        rolled = pltpu.roll(here[c][h], (-shift) % 128, 1)
+                        other = h + (1 if shift > 0 else -1)
+                        if 0 <= other < halves:
+                            rest = pltpu.roll(here[c][other], (-shift) % 128, 1)
+                        else:
+                            rest = 0.0
+                        inside = top[count - 1] if shift > 0 else bottom[count - 1]
+                        return jnp.where(inside, rolled, rest)
+
+                    def at(axis, shift):
+                        if axis == 0:
+                            return padded[c, h, x + 2 + shift, y : y + 8, :]
+                        if axis == 1:
+                            return padded[c, h, x + 2, y + shift : y + shift + 8, :]
+                        return along_z(shift)
+
+                    for axis in range(3):
+                        a1, b1, a2, b2 = (at(axis, shift) for shift in (1, -1, 2, -2))
+                        slope = 8.0 * (a1 - b1) - (a2 - b2)
+                        if axis == 0:
+                            near, far = a1 + b1, a2 + b2
+                            advect = speed[axis] * slope
+                        else:
+                            near, far = near + (a1 + b1), far + (a2 + b2)
+                            advect = advect + speed[axis] * slope
+                    spread = 16.0 * near - far - 90.0 * here[c][h]
+                    rows = slice(8 * tile, 8 * tile + 8)
+                    emit((c, x, rows, lanes), here[c][h], visc * spread - advect)
         return carry
 
     lax.fori_loop(0, nx, plane, 0)
@@ -183,7 +207,7 @@
 
 
 def first_kernel(
-    velocity_ref, viscosity_ref, xlo_ref, xhi_ref, ylo_ref, yhi_ref, match_ref, dest_ref,
+    velocity_ref, viscosity_ref, xa_ref, xb_ref, ya_ref, yb_ref, match_ref, dest_ref,
     base_ref, samples_ref, rank_ref, padded, split, picked,
 ):
     points = match_ref.shape[0] * match_ref.shape[1]
@@ -205,12 +229,24 @@
         running = jnp.dot(both, table, preferred_element_type=F32)
         rank_ref[0:1, start : start + width] = jnp.sum(hot * running, axis=0, keepdims=True)
         earlier = earlier + hot
-    fill_padded(padded, velocity_ref, xlo_ref, xhi_ref, ylo_ref, yhi_ref)
-
-    def emit(c, x, y, here, rate):
-        base_ref[c, x, y : y + 8, :] = here + TIME_STEP * rate
-
-    stencil(padded, viscosity_ref, emit)
+    fill_padded(padded, velocity_ref, xa_ref, xb_ref, ya_ref, yb_ref)
+
+    def emit(spot, here, change):
+        base_ref[spot] = here + change
+
+    stencil(padded, viscosity_ref, TIME_STEP, emit)
+
+
+def faces_of(field_ref, xa_ref, xb_ref, ya_ref, yb_ref):
+    comps, nx, ny, _ = field_ref.shape
+    spot = jnp.where(even_side("region"), nx - 2, 0)
+    even_y = even_side("blk")
+    for c in range(comps):
+        xa_ref[c] = field_ref[c, pl.ds(spot, 2)]
+        xb_ref[c] = field_ref[c, pl.ds(nx - 2 - spot, 2)]
+        low, high = field_ref[c, :, 0:2, :], field_ref[c, :, ny - 2 : ny, :]
+        ya_ref[c] = jnp.where(even_y, high, low)
+        yb_ref[c] = jnp.where(even_y, low, high)
 
 
 def live_row(count_ref, points):
@@ -219,7 +255,7 @@
 
 def stress_kernel(
     count_ref, arrived_ref, dest_ref, wall_ref, rank_ref, samples_ref, base_ref,
-    first_ref, xlow_ref, xhigh_ref, ylow_ref, yhigh_ref, geometry_ref,
+    first_ref, xa_ref, xb_ref, ya_ref, yb_ref, geometry_ref,
 ):
     comps, nx, ny, nz = base_ref.shape
     devices, fields = arrived_ref.shape
@@ -256,10 +292,7 @@
     for c in range(comps):
         block = force[:, c * nz : (c + 1) * nz] * (TIME_STEP / WALL_DY)
         first_ref[c] = base_ref[c] + block.reshape(nx, ny, nz)
-        xlow_ref[c] = first_ref[c, 0:2]
-        xhigh_ref[c] = first_ref[c, nx - 2 : nx]
-        ylow_ref[c] = first_ref[c, :, 0:2, :]
-        yhigh_ref[c] = first_ref[c, :, ny - 2 : ny, :]
+    faces_of(first_ref, xa_ref, xb_ref, ya_ref, yb_ref)
 
 
 def second_kernel(
@@ -283,36 +316,40 @@
 
 
 def last_kernel(
-    velocity_ref, viscosity_ref, first_ref, force_ref, xlo_ref, xhi_ref, ylo_ref, yhi_ref,
+    velocity_ref, viscosity_ref, first_ref, force_ref, xa_ref, xb_ref, ya_ref, yb_ref,
     advanced_ref, padded,
 ):
-    fill_padded(padded, first_ref, xlo_ref, xhi_ref, ylo_ref, yhi_ref)
-
-    def emit(c, x, y, here, rate):
-        rows = slice(y, y + 8)
-        mean = 0.5 * (velocity_ref[c, x, rows, :] + here)
-        advanced_ref[c, x, rows, :] = mean + (
-            0.5 * TIME_STEP * rate + force_ref[c, x, rows, :]
-        )
-
-    stencil(padded, viscosity_ref, emit)
-
-
-def ring(axis, step):
-    count = lax.axis_size(axis)
-    return [(i, (i + step) % count) for i in range(count)]
-
-
-def shift(block, axis, step):
-    return lax.ppermute(block, axis, ring(axis, step))
-
-
-def exchange(xlow, xhigh, ylow, yhigh):
+    fill_padded(padded, first_ref, xa_ref, xb_ref, ya_ref, yb_ref)
+
+    def emit(spot, here, change):
+        advanced_ref[spot] = 0.5 * (velocity_ref[spot] + here) + (change + force_ref[spot])
+
+    stencil(padded, viscosity_ref, 0.5 * TIME_STEP, emit)
+
+
+def exchange(faces):
+    regions, blocks = lax.axis_size("region"), lax.axis_size("blk")
+
+    def swap(block, partner):
+        pairs = []
+        for r in range(regions):
+            for b in range(blocks):
+                to_r, to_b = partner(r, b)
+                pairs.append((r * blocks + b, to_r * blocks + to_b))
+        return lax.ppermute(block, ("region", "blk"), pairs)
+
+    def x_far(r, b):
+        return (r, b ^ 1) if r in (0, regions - 1) else (((r - 1) ^ 1) + 1, b)
+
+    def y_far(r, b):
+        return (r ^ 1, b) if b in (0, blocks - 1) else (r, ((b - 1) ^ 1) + 1)
+
+    xa, xb, ya, yb = faces
     return (
-        shift(xhigh, "region", 1),
-        shift(xlow, "region", -1),
-        shift(yhigh, "blk", 1),
-        shift(ylow, "blk", -1),
+        swap(xa, lambda r, b: (r ^ 1, b)),
+        swap(xb, x_far),
+        swap(ya, lambda r, b: (r, b ^ 1)),
+        swap(yb, y_far),
     )
 
 
@@ -330,24 +367,30 @@
     wall = wall_cell.reshape(square)
     dest = match_dest.reshape(square)
     vmem = pl.BlockSpec(memory_space=pltpu.VMEM)
+    limit = pltpu.CompilerParams(vmem_limit_bytes=24 * 1024 * 1024)
     smem = pl.BlockSpec(memory_space=pltpu.SMEM)
-    padded = pltpu.VMEM((comps, nx + 4, ny + 16, nz), F32)
+    padded = pltpu.VMEM((comps, nz // 128, nx + 4, ny + 16, 128), F32)
     split = pltpu.VMEM((comps * nx * ny, PIECES * nz), BF16)
     picked = pltpu.VMEM((comps * nx * ny, 256), F32)
 
     outgoing = wall_geom.reshape(4, devices, capacity).transpose(1, 0, 2).reshape(devices, -1)
-    arrived = lax.all_to_all(
-        outgoing, ("region", "blk"), split_axis=0, concat_axis=0, tiled=True
-    )
-    halos = exchange(
-        velocity[:, 0:2], velocity[:, nx - 2 :], velocity[:, :, 0:2], velocity[:, :, ny - 2 :]
-    )
+    arrived = lax.all_to_all(outgoing, ("region", "blk"), split_axis=0, concat_axis=0, tiled=True)
+    faces = pl.pallas_call(
+        faces_of,
+        out_shape=(xface, xface, yface, yface),
+        in_specs=[vmem],
+        out_specs=(vmem,) * 4,
+        compiler_params=limit,
+        name="faces",
+    )(velocity)
+    halos = exchange(faces)
     base, samples, rank = pl.pallas_call(
         first_kernel,
         out_shape=(field, rowed, jax.ShapeDtypeStruct((1, points), F32)),
         in_specs=[vmem] * 8,
         out_specs=(vmem,) * 3,
         scratch_shapes=[padded, split, picked],
+        compiler_params=limit,
         name="first",
     )(velocity, viscosity, *halos, match, dest)
     first, *faces, geometry = pl.pallas_call(
@@ -355,15 +398,17 @@
         out_shape=(field, xface, xface, yface, yface, rowed),
         in_specs=[smem] + [vmem] * 6,
         out_specs=(vmem,) * 6,
+        compiler_params=limit,
         name="stress",
     )(match_count, arrived, dest, wall, rank, samples, base)
-    halos = exchange(*faces)
+    halos = exchange(faces)
     force, log_stress = pl.pallas_call(
         second_kernel,
         out_shape=(field, jax.ShapeDtypeStruct(square, F32)),
         in_specs=[smem] + [vmem] * 4,
         out_specs=(vmem,) * 2,
         scratch_shapes=[split, picked],
+        compiler_params=limit,
         name="second",
     )(match_count, first, match, wall, geometry)
     advanced = pl.pallas_call(
@@ -372,6 +417,7 @@
         in_specs=[vmem] * 8,
         out_specs=vmem,
         scratch_shapes=[padded],
+        compiler_params=limit,
         name="last",
     )(velocity, viscosity, first, force, *halos)
     return (advanced, log_stress.reshape(points))

time: 68.4 us -> 46.7 us (0.68)
  the two profiles are of different devices: /device:TPU:0 before, /device:TPU:1 now
where the time goes in v1:
time: 46.7 us; the launch traced here: 46.4 us
  Pallas kernels  18.2 us (39%)
  starting transfers between devices  17.3 us (37%)
  local copies, waits for them, and re-layouts  7.35 us (16%)
  waiting for transfers between devices  2.15 us (5%)
  between operations  1.44 us (3%)
    all_to_all x1, starting transfers between devices, local(): lax.all_to_all(outgoing, ('region', 'blk'), split_axis=0, concat_axis=0,...  9.68 us
    ppermute x8, starting transfers between devices, swap(): return lax.ppermute(block, ('region', 'blk'), pairs)  7.58 us
    pallas_call x1, Pallas kernels, local(): pl.pallas_call(first_kernel, out_shape=(field, rowed, jax.ShapeDtypeStruc...  5.57 us
    pallas_call x1, Pallas kernels, local(): pl.pallas_call(second_kernel, out_shape=(field, jax.ShapeDtypeStruct(squa...  5.21 us
    pallas_call x1, Pallas kernels, local(): pl.pallas_call(last_kernel, out_shape=field, in_specs=[vmem] * 8, out_spe...  4.56 us
    unnamed x16, local copies, waits for them, and re-layouts  3.97 us
    pallas_call x1, Pallas kernels, local(): pl.pallas_call(stress_kernel, out_shape=(field, xface, xface, yface, yfac...  2.71 us
    all_to_all x1, waiting for transfers between devices, local(): lax.all_to_all(outgoing, ('region', 'blk'), split_axis=0, concat_axis=0,...  2.13 us
  transfers between devices with their start and end apart: 9, of which 1 were waited for; matrix products, arithmetic and copies ran while one was open for 7% of the time, Pallas kernels for 23%

profile of v1, /device:TPU:1, one launch (start us, length us, event | category | flops | bytes accessed | tf_op | source)
XLA Modules:
  0.0 46.4 jit_solution(5437252056264824047)
XLA Ops:
  0.6 1.4 %copy-done = f32[3,16,32,256]{3,2,1,0:T(8,128)S(1)} copy-done((f32[3,16,32,256]{3,2,1,0:T(8,128)S(1)}, f32[3,16,32,256]{3,2,1,0:T(8,128)}, u32[]{:S(2)}) %copy-start) | copy-done | bytes 1572888
  2.1 0.1 faces.1
  2.2 1.5 %collective-permute-start = (f32[3,2,32,256]{3,2,1,0:T(8,128)S(1)}, f32[3,2,32,256]{3,2,1,0:T(8,128)S(1)}, u32[]{:S(2)}, u32[]{:S(2)}) collective-permute-start(f32[3,2,32,256]{3,2,1,0:T(8,128)S(1)} %get-tuple-element.17), channel_id=1, source_target_pairs={{0,16},{1,17},{2,18},{3,19},{4,20},{5,21},{6,22},{7,23},{8,24},{9,... | collective-permute-start | bytes 589832 | tf_op jit(solution)/shard_map/ppermute | solution.py:339
  3.6 1.3 %collective-permute-start.1 = (f32[3,2,32,256]{3,2,1,0:T(8,128)S(1)}, f32[3,2,32,256]{3,2,1,0:T(8,128)S(1)}, u32[]{:S(2)}, u32[]{:S(2)}) collective-permute-start(f32[3,2,32,256]{3,2,1,0:T(8,128)S(1)} %get-tuple-element.18), channel_id=1, source_target_pairs={{0,1},{1,0},{2,3},{3,2},{4,5},{5,4},{6,7},{7,6},{8,9},{9,8},{10,11... | collective-permute-start | bytes 589832 | tf_op jit(solution)/shard_map/ppermute | solution.py:339
  4.9 1.6 %collective-permute-start.2 = (f32[3,16,2,256]{3,2,1,0:T(2,128)S(1)}, f32[3,16,2,256]{3,2,1,0:T(2,128)S(1)}, u32[]{:S(2)}, u32[]{:S(2)}) collective-permute-start(f32[3,16,2,256]{3,2,1,0:T(2,128)S(1)} %get-tuple-element.19), channel_id=1, source_target_pairs={{0,1},{1,0},{2,3},{3,2},{4,5},{5,4},{6,7},{7,6},{8,9},{9,8},{10,11... | collective-permute-start | bytes 294920 | tf_op jit(solution)/shard_map/ppermute | solution.py:339
  6.6 0.0 collective-permute-start.3
  6.6 1.6 %reshape.23 = f32[4,128,16]{2,1,0:T(8,128)} reshape(f32[4,2048]{1,0:T(4,128)} %param.13) | data formatting | bytes 65536 | tf_op jit(solution)/shard_map/reshape | solution.py:376
  8.2 1.1 %copy.12 = f32[128,4,16]{0,2,1:T(8,128)S(1)} copy(f32[128,4,16]{2,0,1:T(8,128)} %bitcast.14) | data formatting | bytes 65536 | tf_op jit(solution)/shard_map/transpose | solution.py:376
  9.2 0.7 %copy.13 = f32[128,1,64]{2,1,0:T(1,128)} copy(f32[128,1,64]{0,2,1:T(8,128)S(1)} %bitcast.15) | data formatting | bytes 65536 | tf_op jit(solution)/shard_map/all_to_all | solution.py:377
  10.0 9.7 %all-to-all-start = ((f32[128,1,64]{2,1,0:T(1,128)}), f32[128,1,64]{2,1,0:T(1,128)S(1)}, u32[]{:S(2)}, u32[]{:S(2)}) async-start(f32[128,1,64]{2,1,0:T(1,128)} %copy.13), calls=%async_computation | async-start | bytes 131072 | tf_op jit(solution)/shard_map/all_to_all | solution.py:377
  20.3 0.0 collective-permute-done.3.yb_ref
  20.3 0.0 collective-permute-done.xa_ref
  20.4 5.6 %first.1 = (f32[3,16,32,256]{3,2,1,0:T(8,128)S(1)}, f32[4,1024]{1,0:T(4,128)S(1)}, f32[1,1024]{1,0:T(1,128)S(1)}) custom-call(f32[3,16,32,256]{3,2,1,0:T(8,128)S(1)} %copy-done.1, f32[16,32,256]{2,1,0:T(8,128)S(1)} %copy-done.2, f32[3,2,32,256]{3,2,1,0:T(8,128)S(1)} %collective-permute-done.xa_ref, f32[3,2,32,256]{3,2,1,0:T(8,128)S(1)} %collective-permute-done.1.xb_ref, ...), custom_call_target="tpu_custom_call" | custom-call | tf_op jit(solution)/shard_map/first/pallas_call | solution.py:387
  26.0 0.0 copy-start.3
  26.0 1.1 %copy-done.3 = f32[3,16,32,256]{3,2,1,0:T(8,128)} copy-done((f32[3,16,32,256]{3,2,1,0:T(8,128)}, f32[3,16,32,256]{3,2,1,0:T(8,128)S(1)}, u32[]{:S(2)}) %copy-start.3) | copy-done | bytes 1572888
  27.1 2.1 %all-to-all-done = f32[128,1,64]{2,1,0:T(1,128)S(1)} async-done(((f32[128,1,64]{2,1,0:T(1,128)}), f32[128,1,64]{2,1,0:T(1,128)S(1)}, u32[]{:S(2)}, u32[]{:S(2)}) %all-to-all-start) | async-done | bytes 32800 | tf_op jit(solution)/shard_map/all_to_all | solution.py:377
  29.3 1.4 %copy-done.4 = f32[3,16,32,256]{3,2,1,0:T(8,128)S(1)} copy-done((f32[3,16,32,256]{3,2,1,0:T(8,128)S(1)}, f32[3,16,32,256]{3,2,1,0:T(8,128)}, u32[]{:S(2)}) %copy-start.4) | copy-done | bytes 1572888
  30.7 2.7 %stress.1 = (f32[3,16,32,256]{3,2,1,0:T(8,128)S(1)}, f32[3,2,32,256]{3,2,1,0:T(8,128)S(1)}, f32[3,2,32,256]{3,2,1,0:T(8,128)S(1)}, f32[3,16,2,256]{3,2,1,0:T(2,1...) custom-call(s32[1]{0:T(128)S(6)} %copy.14.count_ref, f32[128,64]{1,0:T(8,128)S(1)} %bitcast.7, ...), custom_call_target="tpu_custom_call" | custom-call | tf_op jit(solution)/shard_map/stress/pallas_call | solution.py:396
  33.4 1.1 %collective-permute-start.4 = (f32[3,2,32,256]{3,2,1,0:T(8,128)S(1)}, f32[3,2,32,256]{3,2,1,0:T(8,128)S(1)}, u32[]{:S(2)}, u32[]{:S(2)}) collective-permute-start(f32[3,2,32,256]{3,2,1,0:T(8,128)S(1)} %get-tuple-element.27), channel_id=1, source_target_pairs={{0,16},{1,17},{2,18},{3,19},{4,20},{5,21},{6,22},{7,23},{8,24},{9,... | collective-permute-start | bytes 589832 | tf_op jit(solution)/shard_map/ppermute | solution.py:339
  34.4 0.3 collective-permute-start.5
  34.7 0.6 %collective-permute-start.6 = (f32[3,16,2,256]{3,2,1,0:T(2,128)S(1)}, f32[3,16,2,256]{3,2,1,0:T(2,128)S(1)}, u32[]{:S(2)}, u32[]{:S(2)}) collective-permute-start(f32[3,16,2,256]{3,2,1,0:T(2,128)S(1)} %get-tuple-element.29), channel_id=1, source_target_pairs={{0,1},{1,0},{2,3},{3,2},{4,5},{5,4},{6,7},{7,6},{8,9},{9,8},{10,11... | collective-permute-start | bytes 294920 | tf_op jit(solution)/shard_map/ppermute | solution.py:339
  35.3 1.3 %collective-permute-start.7 = (f32[3,16,2,256]{3,2,1,0:T(2,128)S(1)}, f32[3,16,2,256]{3,2,1,0:T(2,128)S(1)}, u32[]{:S(2)}, u32[]{:S(2)}) collective-permute-start(f32[3,16,2,256]{3,2,1,0:T(2,128)S(1)} %get-tuple-element.30), channel_id=1, source_target_pairs={{0,16},{1,2},{2,1},{3,4},{4,3},{5,6},{6,5},{7,8},{8,7},{9,10},{10,... | collective-permute-start | bytes 294920 | tf_op jit(solution)/shard_map/ppermute | solution.py:339
  36.5 5.2 %second.1 = (f32[3,16,32,256]{3,2,1,0:T(8,128)S(1)}, f32[8,128]{1,0:T(8,128)}) custom-call(s32[1]{0:T(128)S(6)} %copy.14.count_ref, f32[3,16,32,256]{3,2,1,0:T(8,128)S(1)} %get-tuple-element.24.first_ref, s32[8,128]{1,0:T(8,128)S(1)} %bitcast.13, s32[8,128]{1,0:T(8,128)S(1)} %bitcast.11, f32[4,1024]{1,0:T(4,128)S(1)} %get-tuple-element.25.geometry_ref), custom_call_target="tpu_custom_call" | custom-call | tf_op jit(solution)/shard_map/second/pallas_call | solution.py:405
  41.8 4.6 %last.1 = f32[3,16,32,256]{3,2,1,0:T(8,128)} custom-call(f32[3,16,32,256]{3,2,1,0:T(8,128)S(1)} %copy-done.1, f32[16,32,256]{2,1,0:T(8,128)S(1)} %copy-done.2, f32[3,16,32,256]{3,2,1,0:T(8,128)S(1)} %get-tuple-element.24.first_ref, f32[3,16,32,256]{3,2,1,0:T(8,128)S(1)} %get-tuple-element.26.force_ref, f32[3,2,32,256]{3,2,1,0:T(8,128)S(1)} %collective-permute-done.4.xa_ref, ...), custom_call_target="tpu_custom_call" | custom-call | tf_op jit(solution)/shard_map/last/pallas_call | solution.py:414
  (18 shorter events, 0.0 us)
Async XLA Ops:
  0.6 1.4 %copy-start = (f32[3,16,32,256]{3,2,1,0:T(8,128)S(1)}, f32[3,16,32,256]{3,2,1,0:T(8,128)}, u32[]{:S(2)}) copy-start(f32[3,16,32,256]{3,2,1,0:T(8,128)} %velocity_ref.3) | copy-start | bytes 4718596
  2.0 18.3 %copy-start.1 = (f32[3,16,32,256]{3,2,1,0:T(8,128)S(1)}, f32[3,16,32,256]{3,2,1,0:T(8,128)}, u32[]{:S(2)}) copy-start(f32[3,16,32,256]{3,2,1,0:T(8,128)} %velocity_ref.3) | copy-start | bytes 4718596
  2.0 18.3 %copy-start.2 = (f32[16,32,256]{2,1,0:T(8,128)S(1)}, f32[16,32,256]{2,1,0:T(8,128)}, u32[]{:S(2)}) copy-start(f32[16,32,256]{2,1,0:T(8,128)} %viscosity_ref.3) | copy-start | bytes 1572868
  2.0 18.3 %copy-start.5 = (s32[1024,1]{0,1:T(1,128)S(1)}, s32[1024,1]{0,1:T(1,128)}, u32[]{:S(2)}) copy-start(s32[1024,1]{0,1:T(1,128)} %param.11) | copy-start | bytes 12292
  2.0 18.3 %copy-start.7 = (s32[1024]{0:T(1024)S(1)}, s32[1024]{0:T(1024)}, u32[]{:S(2)}) copy-start(s32[1024]{0:T(1024)} %param.9) | copy-start | bytes 12292
  2.2 18.1 %collective-permute-start = (f32[3,2,32,256]{3,2,1,0:T(8,128)S(1)}, f32[3,2,32,256]{3,2,1,0:T(8,128)S(1)}, u32[]{:S(2)}, u32[]{:S(2)}) collective-permute-start(f32[3,2,32,256]{3,2,1,0:T(8,128)S(1)} %get-tuple-element.17), channel_id=1, source_target_pairs={{0,16},{1,17},{2,18},{3,19},{4,20},{5,21},{6,22},{7,23},{8,24},{9,... | collective-permute-start | bytes 589832 | tf_op jit(solution)/shard_map/ppermute | solution.py:339
  3.6 16.7 %collective-permute-start.1 = (f32[3,2,32,256]{3,2,1,0:T(8,128)S(1)}, f32[3,2,32,256]{3,2,1,0:T(8,128)S(1)}, u32[]{:S(2)}, u32[]{:S(2)}) collective-permute-start(f32[3,2,32,256]{3,2,1,0:T(8,128)S(1)} %get-tuple-element.18), channel_id=1, source_target_pairs={{0,1},{1,0},{2,3},{3,2},{4,5},{5,4},{6,7},{7,6},{8,9},{9,8},{10,11... | collective-permute-start | bytes 589832 | tf_op jit(solution)/shard_map/ppermute | solution.py:339
  4.9 15.4 %collective-permute-start.2 = (f32[3,16,2,256]{3,2,1,0:T(2,128)S(1)}, f32[3,16,2,256]{3,2,1,0:T(2,128)S(1)}, u32[]{:S(2)}, u32[]{:S(2)}) collective-permute-start(f32[3,16,2,256]{3,2,1,0:T(2,128)S(1)} %get-tuple-element.19), channel_id=1, source_target_pairs={{0,1},{1,0},{2,3},{3,2},{4,5},{5,4},{6,7},{7,6},{8,9},{9,8},{10,11... | collective-permute-start | bytes 294920 | tf_op jit(solution)/shard_map/ppermute | solution.py:339
  6.6 13.7 %collective-permute-start.3 = (f32[3,16,2,256]{3,2,1,0:T(2,128)S(1)}, f32[3,16,2,256]{3,2,1,0:T(2,128)S(1)}, u32[]{:S(2)}, u32[]{:S(2)}) collective-permute-start(f32[3,16,2,256]{3,2,1,0:T(2,128)S(1)} %get-tuple-element.20), channel_id=1, source_target_pairs={{0,16},{1,2},{2,1},{3,4},{4,3},{5,6},{6,5},{7,8},{8,7},{9,10},{10,... | collective-permute-start | bytes 294920 | tf_op jit(solution)/shard_map/ppermute | solution.py:339
  8.2 21.1 %copy-start.6 = (s32[1024]{0:T(1024)S(1)}, s32[1024]{0:T(1024)}, u32[]{:S(2)}) copy-start(s32[1024]{0:T(1024)} %param.10) | copy-start | bytes 12292
  10.0 19.3 %all-to-all-start = ((f32[128,1,64]{2,1,0:T(1,128)}), f32[128,1,64]{2,1,0:T(1,128)S(1)}, u32[]{:S(2)}, u32[]{:S(2)}) async-start(f32[128,1,64]{2,1,0:T(1,128)} %copy.13), calls=%async_computation | async-start | bytes 131072 | tf_op jit(solution)/shard_map/all_to_all | solution.py:377
  26.0 1.1 %copy-start.3 = (f32[3,16,32,256]{3,2,1,0:T(8,128)}, f32[3,16,32,256]{3,2,1,0:T(8,128)S(1)}, u32[]{:S(2)}) copy-start(f32[3,16,32,256]{3,2,1,0:T(8,128)S(1)} %get-tuple-element.23.base_ref) | copy-start | bytes 4718596
  29.2 1.4 %copy-start.4 = (f32[3,16,32,256]{3,2,1,0:T(8,128)S(1)}, f32[3,16,32,256]{3,2,1,0:T(8,128)}, u32[]{:S(2)}) copy-start(f32[3,16,32,256]{3,2,1,0:T(8,128)} %copy-done.3) | copy-start | bytes 4718596
  33.4 8.4 %collective-permute-start.4 = (f32[3,2,32,256]{3,2,1,0:T(8,128)S(1)}, f32[3,2,32,256]{3,2,1,0:T(8,128)S(1)}, u32[]{:S(2)}, u32[]{:S(2)}) collective-permute-start(f32[3,2,32,256]{3,2,1,0:T(8,128)S(1)} %get-tuple-element.27), channel_id=1, source_target_pairs={{0,16},{1,17},{2,18},{3,19},{4,20},{5,21},{6,22},{7,23},{8,24},{9,... | collective-permute-start | bytes 589832 | tf_op jit(solution)/shard_map/ppermute | solution.py:339
  34.4 7.4 %collective-permute-start.5 = (f32[3,2,32,256]{3,2,1,0:T(8,128)S(1)}, f32[3,2,32,256]{3,2,1,0:T(8,128)S(1)}, u32[]{:S(2)}, u32[]{:S(2)}) collective-permute-start(f32[3,2,32,256]{3,2,1,0:T(8,128)S(1)} %get-tuple-element.28), channel_id=1, source_target_pairs={{0,1},{1,0},{2,3},{3,2},{4,5},{5,4},{6,7},{7,6},{8,9},{9,8},{10,11... | collective-permute-start | bytes 589832 | tf_op jit(solution)/shard_map/ppermute | solution.py:339
  34.7 7.1 %collective-permute-start.6 = (f32[3,16,2,256]{3,2,1,0:T(2,128)S(1)}, f32[3,16,2,256]{3,2,1,0:T(2,128)S(1)}, u32[]{:S(2)}, u32[]{:S(2)}) collective-permute-start(f32[3,16,2,256]{3,2,1,0:T(2,128)S(1)} %get-tuple-element.29), channel_id=1, source_target_pairs={{0,1},{1,0},{2,3},{3,2},{4,5},{5,4},{6,7},{7,6},{8,9},{9,8},{10,11... | collective-permute-start | bytes 294920 | tf_op jit(solution)/shard_map/ppermute | solution.py:339
  35.3 6.5 %collective-permute-start.7 = (f32[3,16,2,256]{3,2,1,0:T(2,128)S(1)}, f32[3,16,2,256]{3,2,1,0:T(2,128)S(1)}, u32[]{:S(2)}, u32[]{:S(2)}) collective-permute-start(f32[3,16,2,256]{3,2,1,0:T(2,128)S(1)} %get-tuple-element.30), channel_id=1, source_target_pairs={{0,16},{1,2},{2,1},{3,4},{4,3},{5,6},{6,5},{7,8},{8,7},{9,10},{10,... | collective-permute-start | bytes 294920 | tf_op jit(solution)/shard_map/ppermute | solution.py:339

commit v2 on v1

--- a/solution.py
+++ b/solution.py
@@ -16,6 +16,8 @@
 GUESS_RATIO = 14.0
 ETAS = 32
 PIECES = 2
+UNROLL = 2
+FIELD_LANES = 64
 F32 = jnp.float32
 BF16 = jnp.bfloat16
 
@@ -71,7 +73,7 @@
             padded[c, h, 2 : 2 + nx, 8 + ny : 10 + ny, :] = high_y[:, :, lanes]
 
 
-def stencil(padded, viscosity_ref, step, emit):
+def stencil(padded, viscosity_ref, step, keep, emit, finish=None):
     comps, halves = padded.shape[:2]
     nx, ny, _ = viscosity_ref.shape
     lane = lax.broadcasted_iota(jnp.int32, (8, 128), 1)
@@ -88,6 +90,8 @@
             for h in range(halves):
                 lanes = slice(128 * h, 128 * h + 128)
                 visc = viscosity_ref[x, 8 * tile : 8 * tile + 8, lanes] * scale
+                visc_near = 16.0 * visc
+                center = keep - 90.0 * visc
                 speed = [here[c][h] * scale for c in range(comps)]
                 for c in range(comps):
 
@@ -118,12 +122,14 @@
                         else:
                             near, far = near + (a1 + b1), far + (a2 + b2)
                             advect = advect + speed[axis] * slope
-                    spread = 16.0 * near - far - 90.0 * here[c][h]
                     rows = slice(8 * tile, 8 * tile + 8)
-                    emit((c, x, rows, lanes), here[c][h], visc * spread - advect)
+                    value = center * here[c][h] + visc_near * near - visc * far - advect
+                    emit((c, x, rows, lanes), value)
+        if finish is not None:
+            finish(x)
         return carry
 
-    lax.fori_loop(0, nx, plane, 0)
+    lax.fori_loop(0, nx, plane, 0, unroll=UNROLL)
 
 
 def sample_at(field_ref, cells, split, picked):
@@ -206,10 +212,7 @@
     return [factor * t for t in tangent], 2.0 * log_speed
 
 
-def first_kernel(
-    velocity_ref, viscosity_ref, xa_ref, xb_ref, ya_ref, yb_ref, match_ref, dest_ref,
-    base_ref, samples_ref, rank_ref, padded, split, picked,
-):
+def sample_kernel(velocity_ref, match_ref, dest_ref, samples_ref, rank_ref, split, picked):
     points = match_ref.shape[0] * match_ref.shape[1]
     cells = as_row(match_ref[...])
     samples = sample_at(velocity_ref, cells, split, picked)
@@ -229,17 +232,51 @@
         running = jnp.dot(both, table, preferred_element_type=F32)
         rank_ref[0:1, start : start + width] = jnp.sum(hot * running, axis=0, keepdims=True)
         earlier = earlier + hot
+
+
+def rate_kernel(
+    velocity_ref, viscosity_ref, xa_ref, xb_ref, ya_ref, yb_ref, base_ref, padded
+):
     fill_padded(padded, velocity_ref, xa_ref, xb_ref, ya_ref, yb_ref)
 
-    def emit(spot, here, change):
-        base_ref[spot] = here + change
-
-    stencil(padded, viscosity_ref, TIME_STEP, emit)
+    def emit(spot, value):
+        base_ref[spot] = value
+
+    stencil(padded, viscosity_ref, TIME_STEP, 1.0, emit)
+
+
+def pair_spot(nx):
+    return jnp.where(even_side("region"), nx - 2, 0)
+
+
+def faces_kernel(velocity_ref, xa_ref, xb_ref, ya_ref, yb_ref, low, high, sems):
+    comps, nx, ny, _ = velocity_ref.shape
+    spot = pair_spot(nx)
+    copies = [
+        pltpu.make_async_copy(source, target, sems.at[index])
+        for index, (source, target) in enumerate(
+            (
+                (velocity_ref.at[:, pl.ds(spot, 2)], xa_ref),
+                (velocity_ref.at[:, pl.ds(nx - 2 - spot, 2)], xb_ref),
+                (velocity_ref.at[:, :, 0:8, :], low),
+                (velocity_ref.at[:, :, ny - 8 : ny, :], high),
+            )
+        )
+    ]
+    for copy in copies:
+        copy.start()
+    for copy in copies:
+        copy.wait()
+    even_y = even_side("blk")
+    for c in range(comps):
+        near, far = high[c, :, 6:8, :], low[c, :, 0:2, :]
+        ya_ref[c] = jnp.where(even_y, near, far)
+        yb_ref[c] = jnp.where(even_y, far, near)
 
 
 def faces_of(field_ref, xa_ref, xb_ref, ya_ref, yb_ref):
     comps, nx, ny, _ = field_ref.shape
-    spot = jnp.where(even_side("region"), nx - 2, 0)
+    spot = pair_spot(nx)
     even_y = even_side("blk")
     for c in range(comps):
         xa_ref[c] = field_ref[c, pl.ds(spot, 2)]
@@ -249,6 +286,24 @@
         yb_ref[c] = jnp.where(even_y, low, high)
 
 
+def pack_kernel(geometry_ref, out_ref):
+    fields, faces = geometry_ref.shape
+    devices = out_ref.shape[0]
+    capacity = faces // devices
+    lane = lax.broadcasted_iota(jnp.int32, (8, 128), 1)
+    for tile in range(devices // 8):
+        rows = None
+        for k in range(fields):
+            line = geometry_ref[k : k + 1, 128 * tile : 128 * tile + 128]
+            wide = jnp.broadcast_to(line, (8, 128))
+            moved = pltpu.roll(wide, capacity, 1, stride=capacity, stride_axis=0)
+            if k > 0:
+                moved = pltpu.roll(moved, k * capacity, 1)
+            rows = moved if rows is None else jnp.where(lane >= k * capacity, moved, rows)
+        for i in range(8):
+            out_ref[8 * tile + 7 - i : 8 * tile + 8 - i, :] = rows[i : i + 1, :]
+
+
 def live_row(count_ref, points):
     return lax.broadcasted_iota(jnp.int32, (1, points), 1) < count_ref[0]
 
@@ -258,13 +313,13 @@
     first_ref, xa_ref, xb_ref, ya_ref, yb_ref, geometry_ref,
 ):
     comps, nx, ny, nz = base_ref.shape
-    devices, fields = arrived_ref.shape
-    capacity = fields // 4
+    devices = arrived_ref.shape[0]
+    capacity = FIELD_LANES // 4
     points = wall_ref.shape[0] * wall_ref.shape[1]
     owners = as_row(dest_ref[...])
     hot = jnp.where(row_iota((devices, points)) == owners, 1.0, 0.0).astype(BF16)
     table = None
-    for part in pieces_of(arrived_ref[...], 3):
+    for part in pieces_of(arrived_ref[:, :FIELD_LANES], 3):
         term = lax.dot_general(
             part, hot, (((0,), (0,)), ((), ())), preferred_element_type=F32
         )
@@ -317,14 +372,28 @@
 
 def last_kernel(
     velocity_ref, viscosity_ref, first_ref, force_ref, xa_ref, xb_ref, ya_ref, yb_ref,
-    advanced_ref, padded,
+    advanced_ref, padded, result, sems,
 ):
     fill_padded(padded, first_ref, xa_ref, xb_ref, ya_ref, yb_ref)
 
-    def emit(spot, here, change):
-        advanced_ref[spot] = 0.5 * (velocity_ref[spot] + here) + (change + force_ref[spot])
-
-    stencil(padded, viscosity_ref, 0.5 * TIME_STEP, emit)
+    def emit(spot, value):
+        result[spot] = value + (0.5 * velocity_ref[spot] + force_ref[spot])
+
+    def copy_of(x):
+        return pltpu.make_async_copy(
+            result.at[:, pl.ds(x, 1)], advanced_ref.at[:, pl.ds(x, 1)], sems.at[x]
+        )
+
+    def finish(x):
+        copy_of(x).start()
+
+    stencil(padded, viscosity_ref, 0.5 * TIME_STEP, 0.5, emit, finish)
+
+    def settle(x, carry):
+        copy_of(x).wait()
+        return carry
+
+    lax.fori_loop(0, result.shape[1], settle, 0)
 
 
 def exchange(faces):
@@ -355,7 +424,7 @@
 
 def local(velocity, viscosity, match_cell, wall_cell, match_dest, match_count, wall_geom):
     devices = lax.axis_size("region") * lax.axis_size("blk")
-    capacity = wall_geom.shape[1] // devices
+    assert 4 * (wall_geom.shape[1] // devices) == FIELD_LANES
     points = match_cell.shape[0]
     comps, nx, ny, nz = velocity.shape
     field = jax.ShapeDtypeStruct(velocity.shape, F32)
@@ -373,26 +442,47 @@
     split = pltpu.VMEM((comps * nx * ny, PIECES * nz), BF16)
     picked = pltpu.VMEM((comps * nx * ny, 256), F32)
 
-    outgoing = wall_geom.reshape(4, devices, capacity).transpose(1, 0, 2).reshape(devices, -1)
-    arrived = lax.all_to_all(outgoing, ("region", "blk"), split_axis=0, concat_axis=0, tiled=True)
+    outgoing = pl.pallas_call(
+        pack_kernel,
+        out_shape=jax.ShapeDtypeStruct((devices, 128), F32),
+        in_specs=[vmem],
+        out_specs=vmem,
+        compiler_params=limit,
+        name="pack",
+    )(wall_geom)
+    arrived = lax.all_to_all(
+        outgoing.reshape(devices, 1, 128),
+        ("region", "blk"), split_axis=0, concat_axis=0, tiled=True,
+    ).reshape(devices, 128)
+    edge = pltpu.VMEM((comps, nx, 8, nz), F32)
     faces = pl.pallas_call(
-        faces_of,
+        faces_kernel,
         out_shape=(xface, xface, yface, yface),
-        in_specs=[vmem],
+        in_specs=[pl.BlockSpec(memory_space=pltpu.HBM)],
         out_specs=(vmem,) * 4,
+        scratch_shapes=[edge, edge, pltpu.SemaphoreType.DMA((4,))],
         compiler_params=limit,
         name="faces",
     )(velocity)
     halos = exchange(faces)
-    base, samples, rank = pl.pallas_call(
-        first_kernel,
-        out_shape=(field, rowed, jax.ShapeDtypeStruct((1, points), F32)),
-        in_specs=[vmem] * 8,
-        out_specs=(vmem,) * 3,
-        scratch_shapes=[padded, split, picked],
-        compiler_params=limit,
-        name="first",
-    )(velocity, viscosity, *halos, match, dest)
+    samples, rank = pl.pallas_call(
+        sample_kernel,
+        out_shape=(rowed, jax.ShapeDtypeStruct((1, points), F32)),
+        in_specs=[vmem] * 3,
+        out_specs=(vmem,) * 2,
+        scratch_shapes=[split, picked],
+        compiler_params=limit,
+        name="sample",
+    )(velocity, match, dest)
+    base = pl.pallas_call(
+        rate_kernel,
+        out_shape=field,
+        in_specs=[vmem] * 6,
+        out_specs=vmem,
+        scratch_shapes=[padded],
+        compiler_params=limit,
+        name="rate",
+    )(velocity, viscosity, *halos)
     first, *faces, geometry = pl.pallas_call(
         stress_kernel,
         out_shape=(field, xface, xface, yface, yface, rowed),
@@ -415,8 +505,10 @@
         last_kernel,
         out_shape=field,
         in_specs=[vmem] * 8,
-        out_specs=vmem,
-        scratch_shapes=[padded],
+        out_specs=pl.BlockSpec(memory_space=pl.ANY),
+        scratch_shapes=[
+            padded, pltpu.VMEM(velocity.shape, F32), pltpu.SemaphoreType.DMA((nx,))
+        ],
         compiler_params=limit,
         name="last",
     )(velocity, viscosity, first, force, *halos)

time: 46.7 us -> 44.5 us (0.953)
  the two profiles are of different devices: /device:TPU:1 before, /device:TPU:24 now
where the time goes in v2:
time: 44.5 us; the launch traced here: 44.2 us
  starting transfers between devices  18.8 us (42%)
  Pallas kernels  17.7 us (40%)
  local copies, waits for them, and re-layouts  5.99 us (13%)
  between operations  1.7 us (4%)
    ppermute x8, starting transfers between devices, swap(): return lax.ppermute(block, ('region', 'blk'), pairs)  12.4 us
    all_to_all x1, starting transfers between devices, local(): lax.all_to_all(outgoing.reshape(devices, 1, 128), ('region', 'blk'), spli...  6.45 us
    unnamed x26, local copies, waits for them, and re-layouts  5.99 us
    pallas_call x1, Pallas kernels, local(): pl.pallas_call(second_kernel, out_shape=(field, jax.ShapeDtypeStruct(squa...  5.22 us
    pallas_call x1, Pallas kernels, local(): pl.pallas_call(last_kernel, out_shape=field, in_specs=[vmem] * 8, out_spe...  3.61 us
    pallas_call x1, Pallas kernels, local(): pl.pallas_call(stress_kernel, out_shape=(field, xface, xface, yface, yfac...  2.69 us
    pallas_call x1, Pallas kernels, local(): pl.pallas_call(rate_kernel, out_shape=field, in_specs=[vmem] * 6, out_spe...  2.59 us
    pallas_call x1, Pallas kernels, local(): pl.pallas_call(sample_kernel, out_shape=(rowed, jax.ShapeDtypeStruct((1,...  2.33 us
  transfers between devices with their start and end apart: 9, of which 0 were waited for; matrix products, arithmetic and copies ran while one was open for 0% of the time, Pallas kernels for 25%

profile of v2, /device:TPU:24, one launch (start us, length us, event | category | flops | bytes accessed | tf_op | source)
XLA Modules:
  0.0 44.2 jit_solution(5046407590872234573)
XLA Ops:
  0.6 1.4 %copy-done = f32[3,16,32,256]{3,2,1,0:T(8,128)S(1)} copy-done((f32[3,16,32,256]{3,2,1,0:T(8,128)S(1)}, f32[3,16,32,256]{3,2,1,0:T(8,128)}, u32[]{:S(2)}) %copy-start) | copy-done | bytes 1572888
  2.0 0.4 faces.1
  2.4 0.1 collective-permute-start
  2.5 2.0 %collective-permute-start.1 = (f32[3,2,32,256]{3,2,1,0:T(8,128)S(1)}, f32[3,2,32,256]{3,2,1,0:T(8,128)S(1)}, u32[]{:S(2)}, u32[]{:S(2)}) collective-permute-start(f32[3,2,32,256]{3,2,1,0:T(8,128)S(1)} %get-tuple-element.19), channel_id=1, source_target_pairs={{0,1},{1,0},{2,3},{3,2},{4,5},{5,4},{6,7},{7,6},{8,9},{9,8},{10,11... | collective-permute-start | bytes 589832 | tf_op jit(solution)/shard_map/ppermute | solution.py:408
  4.5 0.1 collective-permute-start.2
  4.6 4.2 %collective-permute-start.3 = (f32[3,16,2,256]{3,2,1,0:T(2,128)S(1)}, f32[3,16,2,256]{3,2,1,0:T(2,128)S(1)}, u32[]{:S(2)}, u32[]{:S(2)}) collective-permute-start(f32[3,16,2,256]{3,2,1,0:T(2,128)S(1)} %get-tuple-element.21), channel_id=1, source_target_pairs={{0,16},{1,2},{2,1},{3,4},{4,3},{5,6},{6,5},{7,8},{8,7},{9,10},{10,... | collective-permute-start | bytes 294920 | tf_op jit(solution)/shard_map/ppermute | solution.py:408
  8.8 0.8 %copy-done.8 = f32[4,2048]{1,0:T(4,128)S(1)} copy-done((f32[4,2048]{1,0:T(4,128)S(1)}, f32[4,2048]{1,0:T(4,128)}, u32[]{:S(2)}) %copy-start.8) | copy-done | bytes 32792
  9.6 0.9 %pack.1 = f32[128,128]{1,0:T(8,128)} custom-call(f32[4,2048]{1,0:T(4,128)S(1)} %copy-done.8), custom_call_target="tpu_custom_call" | custom-call | tf_op jit(solution)/shard_map/pack/pallas_call | solution.py:445
  10.5 6.4 %all-to-all-start = ((f32[128,1,128]{2,1,0:T(1,128)}), f32[128,1,128]{2,1,0:T(1,128)S(1)}, u32[]{:S(2)}, u32[]{:S(2)}) async-start(f32[128,1,128]{2,1,0:T(1,128)} %bitcast.1), calls=%async_computation | async-start | bytes 131072 | tf_op jit(solution)/shard_map/all_to_all | solution.py:453
  17.7 0.0 copy-start.11
  17.7 0.7 %copy-done.11 = s32[1024]{0:T(1024)S(1)} copy-done((s32[1024]{0:T(1024)S(1)}, s32[1024]{0:T(1024)}, u32[]{:S(2)}) %copy-start.11) | copy-done | bytes 4120
  18.3 2.3 %sample.1 = (f32[4,1024]{1,0:T(4,128)S(1)}, f32[1,1024]{1,0:T(1,128)S(1)}) custom-call(f32[3,16,32,256]{3,2,1,0:T(8,128)S(1)} %copy-done.1, s32[8,128]{1,0:T(8,128)S(1)} %bitcast.13, s32[8,128]{1,0:T(8,128)S(1)} %bitcast.9), custom_call_target="tpu_custom_call" | custom-call | tf_op jit(solution)/shard_map/sample/pallas_call | solution.py:468
  20.7 0.6 %copy-done.6 = f32[3,16,2,256]{3,2,1,0:T(2,128)} copy-done((f32[3,16,2,256]{3,2,1,0:T(2,128)}, f32[3,16,2,256]{3,2,1,0:T(2,128)S(1)}, u32[]{:S(2)}) %copy-start.6) | copy-done | bytes 98328
  21.4 0.7 %copy-done.4 = f32[3,2,32,256]{3,2,1,0:T(8,128)} copy-done((f32[3,2,32,256]{3,2,1,0:T(8,128)}, f32[3,2,32,256]{3,2,1,0:T(8,128)S(1)}, u32[]{:S(2)}) %copy-start.4) | copy-done | bytes 196632
  22.0 0.9 %copy-done.5 = f32[3,2,32,256]{3,2,1,0:T(8,128)S(1)} copy-done((f32[3,2,32,256]{3,2,1,0:T(8,128)S(1)}, f32[3,2,32,256]{3,2,1,0:T(8,128)}, u32[]{:S(2)}) %copy-start.5) | copy-done | bytes 196632
  23.0 0.9 %copy-done.7 = f32[3,16,2,256]{3,2,1,0:T(2,128)S(1)} copy-done((f32[3,16,2,256]{3,2,1,0:T(2,128)S(1)}, f32[3,16,2,256]{3,2,1,0:T(2,128)}, u32[]{:S(2)}) %copy-start.7) | copy-done | bytes 98328
  23.8 2.6 %rate.1.base_ref = f32[3,16,32,256]{3,2,1,0:T(8,128)S(1)} custom-call(f32[3,16,32,256]{3,2,1,0:T(8,128)S(1)} %copy-done.1, f32[16,32,256]{2,1,0:T(8,128)S(1)} %copy-done.2, f32[3,2,32,256]{3,2,1,0:T(8,128)S(1)} %collective-permute-done.xa_ref, f32[3,2,32,256]{3,2,1,0:T(8,128)S(1)} %copy-done.5, f32[3,16,2,256]{3,2,1,0:T(2,128)S(1)} %collective-permute-done.2.ya_ref, ...), custom_call_target="tpu_custom_call" | custom-call | tf_op jit(solution)/shard_map/rate/pallas_call | solution.py:477
  26.5 2.7 %stress.1 = (f32[3,16,32,256]{3,2,1,0:T(8,128)S(1)}, f32[3,2,32,256]{3,2,1,0:T(8,128)S(1)}, f32[3,2,32,256]{3,2,1,0:T(8,128)S(1)}, f32[3,16,2,256]{3,2,1,0:T(2,1...) custom-call(s32[1]{0:T(128)S(6)} %copy.10.count_ref, f32[128,128]{1,0:T(8,128)S(1)} %bitcast.8, ...), custom_call_target="tpu_custom_call" | custom-call | tf_op jit(solution)/shard_map/stress/pallas_call | solution.py:486
  29.2 0.2 collective-permute-start.4
  29.4 1.7 %collective-permute-start.5 = (f32[3,2,32,256]{3,2,1,0:T(8,128)S(1)}, f32[3,2,32,256]{3,2,1,0:T(8,128)S(1)}, u32[]{:S(2)}, u32[]{:S(2)}) collective-permute-start(f32[3,2,32,256]{3,2,1,0:T(8,128)S(1)} %get-tuple-element.26), channel_id=1, source_target_pairs={{0,1},{1,0},{2,3},{3,2},{4,5},{5,4},{6,7},{7,6},{8,9},{9,8},{10,11... | collective-permute-start | bytes 589832 | tf_op jit(solution)/shard_map/ppermute | solution.py:408
  31.1 0.3 collective-permute-start.6
  31.4 3.7 %collective-permute-start.7 = (f32[3,16,2,256]{3,2,1,0:T(2,128)S(1)}, f32[3,16,2,256]{3,2,1,0:T(2,128)S(1)}, u32[]{:S(2)}, u32[]{:S(2)}) collective-permute-start(f32[3,16,2,256]{3,2,1,0:T(2,128)S(1)} %get-tuple-element.28), channel_id=1, source_target_pairs={{0,16},{1,2},{2,1},{3,4},{4,3},{5,6},{6,5},{7,8},{8,7},{9,10},{10,... | collective-permute-start | bytes 294920 | tf_op jit(solution)/shard_map/ppermute | solution.py:408
  35.1 5.2 %second.1 = (f32[3,16,32,256]{3,2,1,0:T(8,128)S(1)}, f32[8,128]{1,0:T(8,128)}) custom-call(s32[1]{0:T(128)S(6)} %copy.10.count_ref, f32[3,16,32,256]{3,2,1,0:T(8,128)S(1)} %get-tuple-element.22.first_ref, s32[8,128]{1,0:T(8,128)S(1)} %bitcast.14, s32[8,128]{1,0:T(8,128)S(1)} %bitcast.12, f32[4,1024]{1,0:T(4,128)S(1)} %get-tuple-element.23.geometry_ref), custom_call_target="tpu_custom_call" | custom-call | tf_op jit(solution)/shard_map/second/pallas_call | solution.py:495
  40.4 3.6 %last.1 = f32[3,16,32,256]{3,2,1,0:T(8,128)} custom-call(f32[3,16,32,256]{3,2,1,0:T(8,128)S(1)} %copy-done.1, f32[16,32,256]{2,1,0:T(8,128)S(1)} %copy-done.3, f32[3,16,32,256]{3,2,1,0:T(8,128)S(1)} %get-tuple-element.22.first_ref, f32[3,16,32,256]{3,2,1,0:T(8,128)S(1)} %get-tuple-element.24.force_ref, f32[3,2,32,256]{3,2,1,0:T(8,128)S(1)} %collective-permute-done.4.xa_ref, ...), custom_call_target="tpu_custom_call" | custom-call | tf_op jit(solution)/shard_map/last/pallas_call | solution.py:504
  (27 shorter events, 0.1 us)
Async XLA Ops:
  0.6 1.4 %copy-start = (f32[3,16,32,256]{3,2,1,0:T(8,128)S(1)}, f32[3,16,32,256]{3,2,1,0:T(8,128)}, u32[]{:S(2)}) copy-start(f32[3,16,32,256]{3,2,1,0:T(8,128)} %velocity_ref.7) | copy-start | bytes 4718596
  2.0 15.6 %copy-start.1 = (f32[3,16,32,256]{3,2,1,0:T(8,128)S(1)}, f32[3,16,32,256]{3,2,1,0:T(8,128)}, u32[]{:S(2)}) copy-start(f32[3,16,32,256]{3,2,1,0:T(8,128)} %velocity_ref.7) | copy-start | bytes 4718596
  2.0 15.6 %copy-start.9 = (s32[1024,1]{0,1:T(1,128)S(1)}, s32[1024,1]{0,1:T(1,128)}, u32[]{:S(2)}) copy-start(s32[1024,1]{0,1:T(1,128)} %param.11) | copy-start | bytes 12292
  2.4 18.9 %collective-permute-start = (f32[3,2,32,256]{3,2,1,0:T(8,128)S(1)}, f32[3,2,32,256]{3,2,1,0:T(8,128)S(1)}, u32[]{:S(2)}, u32[]{:S(2)}) collective-permute-start(f32[3,2,32,256]{3,2,1,0:T(8,128)S(1)} %get-tuple-element.18), channel_id=1, source_target_pairs={{0,16},{1,17},{2,18},{3,19},{4,20},{5,21},{6,22},{7,23},{8,24},{9,... | collective-permute-start | bytes 589832 | tf_op jit(solution)/shard_map/ppermute | solution.py:408
  2.5 18.8 %collective-permute-start.1 = (f32[3,2,32,256]{3,2,1,0:T(8,128)S(1)}, f32[3,2,32,256]{3,2,1,0:T(8,128)S(1)}, u32[]{:S(2)}, u32[]{:S(2)}) collective-permute-start(f32[3,2,32,256]{3,2,1,0:T(8,128)S(1)} %get-tuple-element.19), channel_id=1, source_target_pairs={{0,1},{1,0},{2,3},{3,2},{4,5},{5,4},{6,7},{7,6},{8,9},{9,8},{10,11... | collective-permute-start | bytes 589832 | tf_op jit(solution)/shard_map/ppermute | solution.py:408
  4.5 16.2 %collective-permute-start.2 = (f32[3,16,2,256]{3,2,1,0:T(2,128)S(1)}, f32[3,16,2,256]{3,2,1,0:T(2,128)S(1)}, u32[]{:S(2)}, u32[]{:S(2)}) collective-permute-start(f32[3,16,2,256]{3,2,1,0:T(2,128)S(1)} %get-tuple-element.20), channel_id=1, source_target_pairs={{0,1},{1,0},{2,3},{3,2},{4,5},{5,4},{6,7},{7,6},{8,9},{9,8},{10,11... | collective-permute-start | bytes 294920 | tf_op jit(solution)/shard_map/ppermute | solution.py:408
  4.6 16.1 %collective-permute-start.3 = (f32[3,16,2,256]{3,2,1,0:T(2,128)S(1)}, f32[3,16,2,256]{3,2,1,0:T(2,128)S(1)}, u32[]{:S(2)}, u32[]{:S(2)}) collective-permute-start(f32[3,16,2,256]{3,2,1,0:T(2,128)S(1)} %get-tuple-element.21), channel_id=1, source_target_pairs={{0,16},{1,2},{2,1},{3,4},{4,3},{5,6},{6,5},{7,8},{8,7},{9,10},{10,... | collective-permute-start | bytes 294920 | tf_op jit(solution)/shard_map/ppermute | solution.py:408
  8.8 0.8 %copy-start.8 = (f32[4,2048]{1,0:T(4,128)S(1)}, f32[4,2048]{1,0:T(4,128)}, u32[]{:S(2)}) copy-start(f32[4,2048]{1,0:T(4,128)} %geometry_ref.1) | copy-start | bytes 98308
  10.5 16.0 %all-to-all-start = ((f32[128,1,128]{2,1,0:T(1,128)}), f32[128,1,128]{2,1,0:T(1,128)S(1)}, u32[]{:S(2)}, u32[]{:S(2)}) async-start(f32[128,1,128]{2,1,0:T(1,128)} %bitcast.1), calls=%async_computation | async-start | bytes 131072 | tf_op jit(solution)/shard_map/all_to_all | solution.py:453
  16.9 5.1 %copy-start.2 = (f32[16,32,256]{2,1,0:T(8,128)S(1)}, f32[16,32,256]{2,1,0:T(8,128)}, u32[]{:S(2)}) copy-start(f32[16,32,256]{2,1,0:T(8,128)} %viscosity_ref.3) | copy-start | bytes 1572868
  17.7 0.7 %copy-start.11 = (s32[1024]{0:T(1024)S(1)}, s32[1024]{0:T(1024)}, u32[]{:S(2)}) copy-start(s32[1024]{0:T(1024)} %param.9) | copy-start | bytes 12292
  18.3 8.1 %copy-start.10 = (s32[1024]{0:T(1024)S(1)}, s32[1024]{0:T(1024)}, u32[]{:S(2)}) copy-start(s32[1024]{0:T(1024)} %param.10) | copy-start | bytes 12292
  20.7 0.6 %copy-start.6 = (f32[3,16,2,256]{3,2,1,0:T(2,128)}, f32[3,16,2,256]{3,2,1,0:T(2,128)S(1)}, u32[]{:S(2)}) copy-start(f32[3,16,2,256]{3,2,1,0:T(2,128)S(1)} %collective-permute-done.3.yb_ref) | copy-start | bytes 294916
  21.3 0.7 %copy-start.4 = (f32[3,2,32,256]{3,2,1,0:T(8,128)}, f32[3,2,32,256]{3,2,1,0:T(8,128)S(1)}, u32[]{:S(2)}) copy-start(f32[3,2,32,256]{3,2,1,0:T(8,128)S(1)} %collective-permute-done.1.xb_ref) | copy-start | bytes 589828
  22.0 0.9 %copy-start.5 = (f32[3,2,32,256]{3,2,1,0:T(8,128)S(1)}, f32[3,2,32,256]{3,2,1,0:T(8,128)}, u32[]{:S(2)}) copy-start(f32[3,2,32,256]{3,2,1,0:T(8,128)} %copy-done.4) | copy-start | bytes 589828
  23.0 0.9 %copy-start.7 = (f32[3,16,2,256]{3,2,1,0:T(2,128)S(1)}, f32[3,16,2,256]{3,2,1,0:T(2,128)}, u32[]{:S(2)}) copy-start(f32[3,16,2,256]{3,2,1,0:T(2,128)} %copy-done.6) | copy-start | bytes 294916
  26.4 8.7 %copy-start.12 = (s32[1024]{0:T(1024)S(1)}, s32[1024]{0:T(1024)}, u32[]{:S(2)}) copy-start(s32[1024]{0:T(1024)} %param.9) | copy-start | bytes 12292
  26.5 13.9 %copy-start.3 = (f32[16,32,256]{2,1,0:T(8,128)S(1)}, f32[16,32,256]{2,1,0:T(8,128)}, u32[]{:S(2)}) copy-start(f32[16,32,256]{2,1,0:T(8,128)} %viscosity_ref.3) | copy-start | bytes 1572868
  29.2 11.2 %collective-permute-start.4 = (f32[3,2,32,256]{3,2,1,0:T(8,128)S(1)}, f32[3,2,32,256]{3,2,1,0:T(8,128)S(1)}, u32[]{:S(2)}, u32[]{:S(2)}) collective-permute-start(f32[3,2,32,256]{3,2,1,0:T(8,128)S(1)} %get-tuple-element.25), channel_id=1, source_target_pairs={{0,16},{1,17},{2,18},{3,19},{4,20},{5,21},{6,22},{7,23},{8,24},{9,... | collective-permute-start | bytes 589832 | tf_op jit(solution)/shard_map/ppermute | solution.py:408
  29.4 11.0 %collective-permute-start.5 = (f32[3,2,32,256]{3,2,1,0:T(8,128)S(1)}, f32[3,2,32,256]{3,2,1,0:T(8,128)S(1)}, u32[]{:S(2)}, u32[]{:S(2)}) collective-permute-start(f32[3,2,32,256]{3,2,1,0:T(8,128)S(1)} %get-tuple-element.26), channel_id=1, source_target_pairs={{0,1},{1,0},{2,3},{3,2},{4,5},{5,4},{6,7},{7,6},{8,9},{9,8},{10,11... | collective-permute-start | bytes 589832 | tf_op jit(solution)/shard_map/ppermute | solution.py:408
  31.1 9.2 %collective-permute-start.6 = (f32[3,16,2,256]{3,2,1,0:T(2,128)S(1)}, f32[3,16,2,256]{3,2,1,0:T(2,128)S(1)}, u32[]{:S(2)}, u32[]{:S(2)}) collective-permute-start(f32[3,16,2,256]{3,2,1,0:T(2,128)S(1)} %get-tuple-element.27), channel_id=1, source_target_pairs={{0,1},{1,0},{2,3},{3,2},{4,5},{5,4},{6,7},{7,6},{8,9},{9,8},{10,11... | collective-permute-start | bytes 294920 | tf_op jit(solution)/shard_map/ppermute | solution.py:408
  31.4 9.0 %collective-permute-start.7 = (f32[3,16,2,256]{3,2,1,0:T(2,128)S(1)}, f32[3,16,2,256]{3,2,1,0:T(2,128)S(1)}, u32[]{:S(2)}, u32[]{:S(2)}) collective-permute-start(f32[3,16,2,256]{3,2,1,0:T(2,128)S(1)} %get-tuple-element.28), channel_id=1, source_target_pairs={{0,16},{1,2},{2,1},{3,4},{4,3},{5,6},{6,5},{7,8},{8,7},{9,10},{10,... | collective-permute-start | bytes 294920 | tf_op jit(solution)/shard_map/ppermute | solution.py:408

commit v3 on v2

--- a/solution.py
+++ b/solution.py
@@ -17,6 +17,7 @@
 ETAS = 32
 PIECES = 2
 UNROLL = 2
+PACK_COST = 4_000_000_000
 FIELD_LANES = 64
 F32 = jnp.float32
 BF16 = jnp.bfloat16
@@ -132,28 +133,29 @@
     lax.fori_loop(0, nx, plane, 0, unroll=UNROLL)
 
 
-def sample_at(field_ref, cells, split, picked):
+def sample_at(field_ref, rows_ref, turns_ref, tiles):
     comps, nx, ny, nz = field_ref.shape
-    points = cells.shape[1]
-    rows = nx * ny
     for c in range(comps):
-        values = field_ref[c].reshape(rows, nz)
-        for index, part in enumerate(pieces_of(values, PIECES)):
-            split[c * rows : (c + 1) * rows, index * nz : (index + 1) * nz] = part
-    lane_cell = cells & (nz - 1)
-    row_cell = cells // nz
-    width = 256
-    sums = [[] for _ in range(comps)]
-    for start in range(0, points, width):
-        lanes = slice(start, start + width)
-        hot = jnp.where(row_iota((nz, width)) == lane_cell[:, lanes], 1.0, 0.0).astype(BF16)
-        hots = jnp.concatenate([hot] * PIECES, axis=0)
-        picked[...] = jnp.dot(split[...], hots, preferred_element_type=F32)
-        mask = row_iota((rows, width)) == row_cell[:, lanes]
-        for c in range(comps):
-            block = picked[c * rows : (c + 1) * rows, :]
-            sums[c].append(jnp.sum(jnp.where(mask, block, 0.0), axis=0, keepdims=True))
-    return [jnp.concatenate(parts, axis=1) for parts in sums]
+        for x in range(nx):
+            for y in range(0, ny, 8):
+                for h in range(nz // 128):
+                    start = ((h * nx + x) * ny + y) * 8 + c
+                    tiles[pl.ds(start, 8, stride=8), :] = field_ref[
+                        c, x, y : y + 8, 128 * h : 128 * h + 128
+                    ]
+    lane = lax.broadcasted_iota(jnp.int32, (8, 128), 1)
+    blocks = []
+    for start in range(0, rows_ref.shape[0], 128):
+        parts = []
+        for low in range(0, 128, 32):
+            part = jnp.zeros((8, 128), F32)
+            for spot in range(low, low + 32):
+                row = pl.multiple_of(rows_ref[start + spot], 8)
+                turned = pltpu.roll(tiles[pl.ds(row, 8), :], turns_ref[start + spot], 1)
+                part = jnp.where(lane == spot, turned, part)
+            parts.append(part)
+        blocks.append((parts[0] + parts[1]) + (parts[2] + parts[3]))
+    return [jnp.concatenate([block[c : c + 1] for block in blocks], axis=1) for c in range(comps)]
 
 
 def scatter_sum(stresses, cells, live, shape):
@@ -212,10 +214,9 @@
     return [factor * t for t in tangent], 2.0 * log_speed
 
 
-def sample_kernel(velocity_ref, match_ref, dest_ref, samples_ref, rank_ref, split, picked):
-    points = match_ref.shape[0] * match_ref.shape[1]
-    cells = as_row(match_ref[...])
-    samples = sample_at(velocity_ref, cells, split, picked)
+def sample_kernel(rows_ref, turns_ref, velocity_ref, dest_ref, samples_ref, rank_ref, tiles):
+    points = rows_ref.shape[0]
+    samples = sample_at(velocity_ref, rows_ref, turns_ref, tiles)
     for c in range(3):
         samples_ref[c : c + 1, :] = samples[c]
     owners = as_row(dest_ref[...])
@@ -249,29 +250,15 @@
     return jnp.where(even_side("region"), nx - 2, 0)
 
 
-def faces_kernel(velocity_ref, xa_ref, xb_ref, ya_ref, yb_ref, low, high, sems):
-    comps, nx, ny, _ = velocity_ref.shape
-    spot = pair_spot(nx)
-    copies = [
-        pltpu.make_async_copy(source, target, sems.at[index])
-        for index, (source, target) in enumerate(
-            (
-                (velocity_ref.at[:, pl.ds(spot, 2)], xa_ref),
-                (velocity_ref.at[:, pl.ds(nx - 2 - spot, 2)], xb_ref),
-                (velocity_ref.at[:, :, 0:8, :], low),
-                (velocity_ref.at[:, :, ny - 8 : ny, :], high),
-            )
-        )
-    ]
-    for copy in copies:
-        copy.start()
-    for copy in copies:
-        copy.wait()
-    even_y = even_side("blk")
-    for c in range(comps):
-        near, far = high[c, :, 6:8, :], low[c, :, 0:2, :]
-        ya_ref[c] = jnp.where(even_y, near, far)
-        yb_ref[c] = jnp.where(even_y, far, near)
+def faces_kernel(
+    velocity_ref, match_ref, xa_ref, xb_ref, ya_ref, yb_ref, rows_ref, turns_ref
+):
+    _, nx, ny, nz = velocity_ref.shape
+    cells = match_ref[...]
+    half, row = (cells // 128) % (nz // 128), cells // nz
+    rows_ref[...] = (half * (nx * ny) + row) * 8
+    turns_ref[...] = (lax.broadcasted_iota(jnp.int32, cells.shape, 1) - cells) & 127
+    faces_of(velocity_ref, xa_ref, xb_ref, ya_ref, yb_ref)
 
 
 def faces_of(field_ref, xa_ref, xb_ref, ya_ref, yb_ref):
@@ -351,11 +338,12 @@
 
 
 def second_kernel(
-    count_ref, first_ref, match_ref, wall_ref, geometry_ref, force_ref, log_ref, split, picked,
+    count_ref, rows_ref, turns_ref, velocity_ref, first_ref, wall_ref, geometry_ref,
+    part_ref, log_ref, tiles,
 ):
     comps, nx, ny, nz = first_ref.shape
-    points = wall_ref.shape[0] * wall_ref.shape[1]
-    samples = sample_at(first_ref, as_row(match_ref[...]), split, picked)
+    points = rows_ref.shape[0]
+    samples = sample_at(first_ref, rows_ref, turns_ref, tiles)
     distance = geometry_ref[0:1, :]
     normals = [geometry_ref[k : k + 1, :] for k in range(1, 4)]
     stress, log_stress = wall_solve(samples, distance, normals)
@@ -367,17 +355,17 @@
     force = scatter_sum(stress, as_row(wall_ref[...]), live, first_ref.shape)
     for c in range(comps):
         block = force[:, c * nz : (c + 1) * nz] * (0.5 * TIME_STEP / WALL_DY)
-        force_ref[c] = block.reshape(nx, ny, nz)
+        part_ref[c] = 0.5 * velocity_ref[c] + block.reshape(nx, ny, nz)
 
 
 def last_kernel(
-    velocity_ref, viscosity_ref, first_ref, force_ref, xa_ref, xb_ref, ya_ref, yb_ref,
+    viscosity_ref, first_ref, part_ref, xa_ref, xb_ref, ya_ref, yb_ref,
     advanced_ref, padded, result, sems,
 ):
     fill_padded(padded, first_ref, xa_ref, xb_ref, ya_ref, yb_ref)
 
     def emit(spot, value):
-        result[spot] = value + (0.5 * velocity_ref[spot] + force_ref[spot])
+        result[spot] = value + part_ref[spot]
 
     def copy_of(x):
         return pltpu.make_async_copy(
@@ -439,41 +427,41 @@
     limit = pltpu.CompilerParams(vmem_limit_bytes=24 * 1024 * 1024)
     smem = pl.BlockSpec(memory_space=pltpu.SMEM)
     padded = pltpu.VMEM((comps, nz // 128, nx + 4, ny + 16, 128), F32)
-    split = pltpu.VMEM((comps * nx * ny, PIECES * nz), BF16)
-    picked = pltpu.VMEM((comps * nx * ny, 256), F32)
-
+    tiles = pltpu.VMEM((8 * nx * ny * (nz // 128), 128), F32)
+
+    spots = jax.ShapeDtypeStruct(square, jnp.int32)
     outgoing = pl.pallas_call(
         pack_kernel,
         out_shape=jax.ShapeDtypeStruct((devices, 128), F32),
         in_specs=[vmem],
         out_specs=vmem,
         compiler_params=limit,
+        cost_estimate=pl.CostEstimate(flops=PACK_COST, bytes_accessed=98304, transcendentals=0),
         name="pack",
     )(wall_geom)
     arrived = lax.all_to_all(
         outgoing.reshape(devices, 1, 128),
         ("region", "blk"), split_axis=0, concat_axis=0, tiled=True,
     ).reshape(devices, 128)
-    edge = pltpu.VMEM((comps, nx, 8, nz), F32)
-    faces = pl.pallas_call(
+    *faces, rows, turns = pl.pallas_call(
         faces_kernel,
-        out_shape=(xface, xface, yface, yface),
-        in_specs=[pl.BlockSpec(memory_space=pltpu.HBM)],
-        out_specs=(vmem,) * 4,
-        scratch_shapes=[edge, edge, pltpu.SemaphoreType.DMA((4,))],
+        out_shape=(xface, xface, yface, yface, spots, spots),
+        in_specs=[vmem] * 2,
+        out_specs=(vmem,) * 6,
         compiler_params=limit,
         name="faces",
-    )(velocity)
+    )(velocity, match)
+    rows, turns = rows.reshape(points), turns.reshape(points)
     halos = exchange(faces)
     samples, rank = pl.pallas_call(
         sample_kernel,
         out_shape=(rowed, jax.ShapeDtypeStruct((1, points), F32)),
-        in_specs=[vmem] * 3,
+        in_specs=[smem] * 2 + [vmem] * 2,
         out_specs=(vmem,) * 2,
-        scratch_shapes=[split, picked],
+        scratch_shapes=[tiles],
         compiler_params=limit,
         name="sample",
-    )(velocity, match, dest)
+    )(rows, turns, velocity, dest)
     base = pl.pallas_call(
         rate_kernel,
         out_shape=field,
@@ -492,26 +480,26 @@
         name="stress",
     )(match_count, arrived, dest, wall, rank, samples, base)
     halos = exchange(faces)
-    force, log_stress = pl.pallas_call(
+    part, log_stress = pl.pallas_call(
         second_kernel,
         out_shape=(field, jax.ShapeDtypeStruct(square, F32)),
-        in_specs=[smem] + [vmem] * 4,
+        in_specs=[smem] * 3 + [vmem] * 4,
         out_specs=(vmem,) * 2,
-        scratch_shapes=[split, picked],
+        scratch_shapes=[tiles],
         compiler_params=limit,
         name="second",
-    )(match_count, first, match, wall, geometry)
+    )(match_count, rows, turns, velocity, first, wall, geometry)
     advanced = pl.pallas_call(
         last_kernel,
         out_shape=field,
-        in_specs=[vmem] * 8,
+        in_specs=[vmem] * 7,
         out_specs=pl.BlockSpec(memory_space=pl.ANY),
         scratch_shapes=[
             padded, pltpu.VMEM(velocity.shape, F32), pltpu.SemaphoreType.DMA((nx,))
         ],
         compiler_params=limit,
         name="last",
-    )(velocity, viscosity, first, force, *halos)
+    )(viscosity, first, part, *halos)
     return (advanced, log_stress.reshape(points))
 
 

time: 44.5 us -> 43.8 us (0.984)
  Pallas kernels: 17.7 us -> 16.6 us
    all_to_all x1, starting transfers between devices: 6.45 us -> 7.67 us  [local(): lax.all_to_all(outgoing.reshape(devices, 1, 128), ('region', 'blk'), spli...]
    ppermute x8, starting transfers between devices: 12.4 us -> 11.5 us  [swap(): return lax.ppermute(block, ('region', 'blk'), pairs)]
    pallas_call x1, Pallas kernels: 5.22 us -> 4.51 us  [local(): pl.pallas_call(second_kernel, out_shape=(field, jax.ShapeDtypeStruct(squa...]
    unnamed x26 -> x24, local copies, waits for them, and re-layouts: 5.99 us -> 6.27 us
  transfers between devices with their start and end apart: 9 -> 9, of which waited for: 0 -> 0; matrix products, arithmetic and copies ran while one was open for 0% -> 0% of each run, Pallas kernels for 25% -> 24%
where the time goes in v3:
time: 43.8 us; the launch traced here: 43.5 us
  starting transfers between devices  19.2 us (44%)
  Pallas kernels  16.6 us (38%)
  local copies, waits for them, and re-layouts  6.27 us (14%)
  between operations  1.44 us (3%)
    ppermute x8, starting transfers between devices, swap(): return lax.ppermute(block, ('region', 'blk'), pairs)  11.5 us
    all_to_all x1, starting transfers between devices, local(): lax.all_to_all(outgoing.reshape(devices, 1, 128), ('region', 'blk'), spli...  7.67 us
    unnamed x24, local copies, waits for them, and re-layouts  6.27 us
    pallas_call x1, Pallas kernels, local(): pl.pallas_call(second_kernel, out_shape=(field, jax.ShapeDtypeStruct(squa...  4.51 us
    pallas_call x1, Pallas kernels, local(): pl.pallas_call(last_kernel, out_shape=field, in_specs=[vmem] * 7, out_spe...  3.45 us
    pallas_call x1, Pallas kernels, local(): pl.pallas_call(stress_kernel, out_shape=(field, xface, xface, yface, yfac...  2.71 us
    pallas_call x1, Pallas kernels, local(): pl.pallas_call(rate_kernel, out_shape=field, in_specs=[vmem] * 6, out_spe...  2.59 us
    pallas_call x1, Pallas kernels, local(): pl.pallas_call(sample_kernel, out_shape=(rowed, jax.ShapeDtypeStruct((1,...  2.41 us
  transfers between devices with their start and end apart: 9, of which 0 were waited for; matrix products, arithmetic and copies ran while one was open for 0% of the time, Pallas kernels for 24%

profile of v3, /device:TPU:24, one launch (start us, length us, event | category | flops | bytes accessed | tf_op | source)
XLA Modules:
  0.0 43.5 jit_solution(7792573887946671457)
XLA Ops:
  0.6 0.0 copy-start
  0.6 1.4 %copy-done = f32[3,16,32,256]{3,2,1,0:T(8,128)S(1)} copy-done((f32[3,16,32,256]{3,2,1,0:T(8,128)S(1)}, f32[3,16,32,256]{3,2,1,0:T(8,128)}, u32[]{:S(2)}) %copy-start) | copy-done | bytes 1572888
  2.0 0.7 %copy-done.10 = s32[1024]{0:T(1024)S(1)} copy-done((s32[1024]{0:T(1024)S(1)}, s32[1024]{0:T(1024)}, u32[]{:S(2)}) %copy-start.10) | copy-done | bytes 4120
  2.7 0.1 faces.1
  2.9 2.0 %collective-permute-start.2 = (f32[3,16,2,256]{3,2,1,0:T(2,128)S(1)}, f32[3,16,2,256]{3,2,1,0:T(2,128)S(1)}, u32[]{:S(2)}, u32[]{:S(2)}) collective-permute-start(f32[3,16,2,256]{3,2,1,0:T(2,128)S(1)} %get-tuple-element.24), channel_id=1, source_target_pairs={{0,1},{1,0},{2,3},{3,2},{4,5},{5,4},{6,7},{7,6},{8,9},{9,8},{10,11... | collective-permute-start | bytes 294920 | tf_op jit(solution)/shard_map/ppermute | solution.py:396
  4.9 2.7 %collective-permute-start.3 = (f32[3,16,2,256]{3,2,1,0:T(2,128)S(1)}, f32[3,16,2,256]{3,2,1,0:T(2,128)S(1)}, u32[]{:S(2)}, u32[]{:S(2)}) collective-permute-start(f32[3,16,2,256]{3,2,1,0:T(2,128)S(1)} %get-tuple-element.25), channel_id=1, source_target_pairs={{0,16},{1,2},{2,1},{3,4},{4,3},{5,6},{6,5},{7,8},{8,7},{9,10},{10,... | collective-permute-start | bytes 294920 | tf_op jit(solution)/shard_map/ppermute | solution.py:396
  7.6 0.8 %collective-permute-start.1 = (f32[3,2,32,256]{3,2,1,0:T(8,128)S(1)}, f32[3,2,32,256]{3,2,1,0:T(8,128)S(1)}, u32[]{:S(2)}, u32[]{:S(2)}) collective-permute-start(f32[3,2,32,256]{3,2,1,0:T(8,128)S(1)} %get-tuple-element.23), channel_id=1, source_target_pairs={{0,1},{1,0},{2,3},{3,2},{4,5},{5,4},{6,7},{7,6},{8,9},{9,8},{10,11... | collective-permute-start | bytes 589832 | tf_op jit(solution)/shard_map/ppermute | solution.py:396
  8.4 0.9 %pack.1 = f32[128,128]{1,0:T(8,128)} custom-call(f32[4,2048]{1,0:T(4,128)S(1)} %copy-done.11), custom_call_target="tpu_custom_call" | custom-call | flops 4000000000 | bytes 98304 | tf_op jit(solution)/shard_map/pack/pallas_call | solution.py:433
  9.3 7.7 %all-to-all-start = ((f32[128,1,128]{2,1,0:T(1,128)}), f32[128,1,128]{2,1,0:T(1,128)S(1)}, u32[]{:S(2)}, u32[]{:S(2)}) async-start(f32[128,1,128]{2,1,0:T(1,128)} %bitcast.1), calls=%async_computation | async-start | bytes 131072 | tf_op jit(solution)/shard_map/all_to_all | solution.py:442
  17.6 0.0 copy-start.9
  17.6 2.4 %sample.1 = (f32[4,1024]{1,0:T(4,128)S(1)}, f32[1,1024]{1,0:T(1,128)S(1)}) custom-call(s32[1024]{0:T(1024)S(1)} %bitcast.15, s32[1024]{0:T(1024)S(1)} %bitcast.17, f32[3,16,32,256]{3,2,1,0:T(8,128)S(1)} %copy-done.1, s32[8,128]{1,0:T(8,128)S(1)} %bitcast.11), custom_call_target="tpu_custom_call" | custom-call | tf_op jit(solution)/shard_map/sample/pallas_call | solution.py:456
  20.1 0.6 %copy-done.6 = f32[3,16,2,256]{3,2,1,0:T(2,128)} copy-done((f32[3,16,2,256]{3,2,1,0:T(2,128)}, f32[3,16,2,256]{3,2,1,0:T(2,128)S(1)}, u32[]{:S(2)}) %copy-start.6) | copy-done | bytes 98328
  20.7 0.7 %copy-done.4 = f32[3,2,32,256]{3,2,1,0:T(8,128)} copy-done((f32[3,2,32,256]{3,2,1,0:T(8,128)}, f32[3,2,32,256]{3,2,1,0:T(8,128)S(1)}, u32[]{:S(2)}) %copy-start.4) | copy-done | bytes 196632
  21.4 1.0 %copy-done.2 = f32[16,32,256]{2,1,0:T(8,128)S(1)} copy-done((f32[16,32,256]{2,1,0:T(8,128)S(1)}, f32[16,32,256]{2,1,0:T(8,128)}, u32[]{:S(2)}) %copy-start.2) | copy-done | bytes 524312
  22.4 0.9 %copy-done.5 = f32[3,2,32,256]{3,2,1,0:T(8,128)S(1)} copy-done((f32[3,2,32,256]{3,2,1,0:T(8,128)S(1)}, f32[3,2,32,256]{3,2,1,0:T(8,128)}, u32[]{:S(2)}) %copy-start.5) | copy-done | bytes 196632
  23.4 0.9 %copy-done.7 = f32[3,16,2,256]{3,2,1,0:T(2,128)S(1)} copy-done((f32[3,16,2,256]{3,2,1,0:T(2,128)S(1)}, f32[3,16,2,256]{3,2,1,0:T(2,128)}, u32[]{:S(2)}) %copy-start.7) | copy-done | bytes 98328
  24.2 2.6 %rate.1.base_ref = f32[3,16,32,256]{3,2,1,0:T(8,128)S(1)} custom-call(f32[3,16,32,256]{3,2,1,0:T(8,128)S(1)} %copy-done.1, f32[16,32,256]{2,1,0:T(8,128)S(1)} %copy-done.2, f32[3,2,32,256]{3,2,1,0:T(8,128)S(1)} %collective-permute-done.xa_ref, f32[3,2,32,256]{3,2,1,0:T(8,128)S(1)} %copy-done.5, f32[3,16,2,256]{3,2,1,0:T(2,128)S(1)} %collective-permute-done.2.ya_ref, ...), custom_call_target="tpu_custom_call" | custom-call | tf_op jit(solution)/shard_map/rate/pallas_call | solution.py:465
  26.9 2.7 %stress.1 = (f32[3,16,32,256]{3,2,1,0:T(8,128)S(1)}, f32[3,2,32,256]{3,2,1,0:T(8,128)S(1)}, f32[3,2,32,256]{3,2,1,0:T(8,128)S(1)}, f32[3,16,2,256]{3,2,1,0:T(2,1...) custom-call(s32[1]{0:T(128)S(6)} %copy.10.count_ref, f32[128,128]{1,0:T(8,128)S(1)} %bitcast.10, ...), custom_call_target="tpu_custom_call" | custom-call | tf_op jit(solution)/shard_map/stress/pallas_call | solution.py:474
  29.6 0.2 collective-permute-start.4
  29.8 1.7 %collective-permute-start.5 = (f32[3,2,32,256]{3,2,1,0:T(8,128)S(1)}, f32[3,2,32,256]{3,2,1,0:T(8,128)S(1)}, u32[]{:S(2)}, u32[]{:S(2)}) collective-permute-start(f32[3,2,32,256]{3,2,1,0:T(8,128)S(1)} %get-tuple-element.30), channel_id=1, source_target_pairs={{0,1},{1,0},{2,3},{3,2},{4,5},{5,4},{6,7},{7,6},{8,9},{9,8},{10,11... | collective-permute-start | bytes 589832 | tf_op jit(solution)/shard_map/ppermute | solution.py:396
  31.5 0.3 collective-permute-start.6
  31.8 3.7 %collective-permute-start.7 = (f32[3,16,2,256]{3,2,1,0:T(2,128)S(1)}, f32[3,16,2,256]{3,2,1,0:T(2,128)S(1)}, u32[]{:S(2)}, u32[]{:S(2)}) collective-permute-start(f32[3,16,2,256]{3,2,1,0:T(2,128)S(1)} %get-tuple-element.32), channel_id=1, source_target_pairs={{0,16},{1,2},{2,1},{3,4},{4,3},{5,6},{6,5},{7,8},{8,7},{9,10},{10,... | collective-permute-start | bytes 294920 | tf_op jit(solution)/shard_map/ppermute | solution.py:396
  35.5 4.5 %second.1 = (f32[3,16,32,256]{3,2,1,0:T(8,128)S(1)}, f32[8,128]{1,0:T(8,128)}) custom-call(s32[1]{0:T(128)S(6)} %copy.10.count_ref, s32[1024]{0:T(1024)S(1)} %bitcast.16, s32[1024]{0:T(1024)S(1)} %bitcast.18, f32[3,16,32,256]{3,2,1,0:T(8,128)S(1)} %copy-done.1, f32[3,16,32,256]{3,2,1,0:T(8,128)S(1)} %get-tuple-element.26.first_ref, s32[8,128]{1,0:T(8,128)S(1)} %bitcast.14, ...), custom_call_target="tpu_custom_call" | custom-call | tf_op jit(solution)/shard_map/second/pallas_call | solution.py:483
  40.1 3.4 %last.1 = f32[3,16,32,256]{3,2,1,0:T(8,128)} custom-call(f32[16,32,256]{2,1,0:T(8,128)S(1)} %copy-done.3, f32[3,16,32,256]{3,2,1,0:T(8,128)S(1)} %get-tuple-element.26.first_ref, f32[3,16,32,256]{3,2,1,0:T(8,128)S(1)} %get-tuple-element.28.part_ref, f32[3,2,32,256]{3,2,1,0:T(8,128)S(1)} %collective-permute-done.4.xa_ref, ...), custom_call_target="tpu_custom_call" | custom-call | tf_op jit(solution)/shard_map/last/pallas_call | solution.py:492
  (25 shorter events, 0.1 us)
Async XLA Ops:
  0.6 1.4 %copy-start = (f32[3,16,32,256]{3,2,1,0:T(8,128)S(1)}, f32[3,16,32,256]{3,2,1,0:T(8,128)}, u32[]{:S(2)}) copy-start(f32[3,16,32,256]{3,2,1,0:T(8,128)} %velocity_ref.7) | copy-start | bytes 4718596
  2.0 0.7 %copy-start.10 = (s32[1024]{0:T(1024)S(1)}, s32[1024]{0:T(1024)}, u32[]{:S(2)}) copy-start(s32[1024]{0:T(1024)} %param.9) | copy-start | bytes 12292
  2.7 5.7 %copy-start.11 = (f32[4,2048]{1,0:T(4,128)S(1)}, f32[4,2048]{1,0:T(4,128)}, u32[]{:S(2)}) copy-start(f32[4,2048]{1,0:T(4,128)} %geometry_ref.1) | copy-start | bytes 98308
  2.9 17.2 %collective-permute-start.2 = (f32[3,16,2,256]{3,2,1,0:T(2,128)S(1)}, f32[3,16,2,256]{3,2,1,0:T(2,128)S(1)}, u32[]{:S(2)}, u32[]{:S(2)}) collective-permute-start(f32[3,16,2,256]{3,2,1,0:T(2,128)S(1)} %get-tuple-element.24), channel_id=1, source_target_pairs={{0,1},{1,0},{2,3},{3,2},{4,5},{5,4},{6,7},{7,6},{8,9},{9,8},{10,11... | collective-permute-start | bytes 294920 | tf_op jit(solution)/shard_map/ppermute | solution.py:396
  4.9 15.2 %collective-permute-start.3 = (f32[3,16,2,256]{3,2,1,0:T(2,128)S(1)}, f32[3,16,2,256]{3,2,1,0:T(2,128)S(1)}, u32[]{:S(2)}, u32[]{:S(2)}) collective-permute-start(f32[3,16,2,256]{3,2,1,0:T(2,128)S(1)} %get-tuple-element.25), channel_id=1, source_target_pairs={{0,16},{1,2},{2,1},{3,4},{4,3},{5,6},{6,5},{7,8},{8,7},{9,10},{10,... | collective-permute-start | bytes 294920 | tf_op jit(solution)/shard_map/ppermute | solution.py:396
  7.6 13.1 %collective-permute-start = (f32[3,2,32,256]{3,2,1,0:T(8,128)S(1)}, f32[3,2,32,256]{3,2,1,0:T(8,128)S(1)}, u32[]{:S(2)}, u32[]{:S(2)}) collective-permute-start(f32[3,2,32,256]{3,2,1,0:T(8,128)S(1)} %get-tuple-element.22), channel_id=1, source_target_pairs={{0,16},{1,17},{2,18},{3,19},{4,20},{5,21},{6,22},{7,23},{8,24},{9,... | collective-permute-start | bytes 589832 | tf_op jit(solution)/shard_map/ppermute | solution.py:396
  7.6 10.0 %copy-start.1 = (f32[3,16,32,256]{3,2,1,0:T(8,128)S(1)}, f32[3,16,32,256]{3,2,1,0:T(8,128)}, u32[]{:S(2)}) copy-start(f32[3,16,32,256]{3,2,1,0:T(8,128)} %velocity_ref.7) | copy-start | bytes 4718596
  7.6 10.0 %copy-start.8 = (s32[1024,1]{0,1:T(1,128)S(1)}, s32[1024,1]{0,1:T(1,128)}, u32[]{:S(2)}) copy-start(s32[1024,1]{0,1:T(1,128)} %param.11) | copy-start | bytes 12292
  7.6 13.1 %collective-permute-start.1 = (f32[3,2,32,256]{3,2,1,0:T(8,128)S(1)}, f32[3,2,32,256]{3,2,1,0:T(8,128)S(1)}, u32[]{:S(2)}, u32[]{:S(2)}) collective-permute-start(f32[3,2,32,256]{3,2,1,0:T(8,128)S(1)} %get-tuple-element.23), channel_id=1, source_target_pairs={{0,1},{1,0},{2,3},{3,2},{4,5},{5,4},{6,7},{7,6},{8,9},{9,8},{10,11... | collective-permute-start | bytes 589832 | tf_op jit(solution)/shard_map/ppermute | solution.py:396
  9.3 17.6 %all-to-all-start = ((f32[128,1,128]{2,1,0:T(1,128)}), f32[128,1,128]{2,1,0:T(1,128)S(1)}, u32[]{:S(2)}, u32[]{:S(2)}) async-start(f32[128,1,128]{2,1,0:T(1,128)} %bitcast.1), calls=%async_computation | async-start | bytes 131072 | tf_op jit(solution)/shard_map/all_to_all | solution.py:442
  17.6 9.2 %copy-start.9 = (s32[1024]{0:T(1024)S(1)}, s32[1024]{0:T(1024)}, u32[]{:S(2)}) copy-start(s32[1024]{0:T(1024)} %param.10) | copy-start | bytes 12292
  20.1 0.6 %copy-start.6 = (f32[3,16,2,256]{3,2,1,0:T(2,128)}, f32[3,16,2,256]{3,2,1,0:T(2,128)S(1)}, u32[]{:S(2)}) copy-start(f32[3,16,2,256]{3,2,1,0:T(2,128)S(1)} %collective-permute-done.3.yb_ref) | copy-start | bytes 294916
  20.7 0.7 %copy-start.4 = (f32[3,2,32,256]{3,2,1,0:T(8,128)}, f32[3,2,32,256]{3,2,1,0:T(8,128)S(1)}, u32[]{:S(2)}) copy-start(f32[3,2,32,256]{3,2,1,0:T(8,128)S(1)} %collective-permute-done.1.xb_ref) | copy-start | bytes 589828
  21.4 1.0 %copy-start.2 = (f32[16,32,256]{2,1,0:T(8,128)S(1)}, f32[16,32,256]{2,1,0:T(8,128)}, u32[]{:S(2)}) copy-start(f32[16,32,256]{2,1,0:T(8,128)} %viscosity_ref.3) | copy-start | bytes 1572868
  22.4 0.9 %copy-start.5 = (f32[3,2,32,256]{3,2,1,0:T(8,128)S(1)}, f32[3,2,32,256]{3,2,1,0:T(8,128)}, u32[]{:S(2)}) copy-start(f32[3,2,32,256]{3,2,1,0:T(8,128)} %copy-done.4) | copy-start | bytes 589828
  23.4 0.9 %copy-start.7 = (f32[3,16,2,256]{3,2,1,0:T(2,128)S(1)}, f32[3,16,2,256]{3,2,1,0:T(2,128)}, u32[]{:S(2)}) copy-start(f32[3,16,2,256]{3,2,1,0:T(2,128)} %copy-done.6) | copy-start | bytes 294916
  29.6 10.5 %collective-permute-start.4 = (f32[3,2,32,256]{3,2,1,0:T(8,128)S(1)}, f32[3,2,32,256]{3,2,1,0:T(8,128)S(1)}, u32[]{:S(2)}, u32[]{:S(2)}) collective-permute-start(f32[3,2,32,256]{3,2,1,0:T(8,128)S(1)} %get-tuple-element.29), channel_id=1, source_target_pairs={{0,16},{1,17},{2,18},{3,19},{4,20},{5,21},{6,22},{7,23},{8,24},{9,... | collective-permute-start | bytes 589832 | tf_op jit(solution)/shard_map/ppermute | solution.py:396
  29.8 10.3 %collective-permute-start.5 = (f32[3,2,32,256]{3,2,1,0:T(8,128)S(1)}, f32[3,2,32,256]{3,2,1,0:T(8,128)S(1)}, u32[]{:S(2)}, u32[]{:S(2)}) collective-permute-start(f32[3,2,32,256]{3,2,1,0:T(8,128)S(1)} %get-tuple-element.30), channel_id=1, source_target_pairs={{0,1},{1,0},{2,3},{3,2},{4,5},{5,4},{6,7},{7,6},{8,9},{9,8},{10,11... | collective-permute-start | bytes 589832 | tf_op jit(solution)/shard_map/ppermute | solution.py:396
  31.5 8.5 %collective-permute-start.6 = (f32[3,16,2,256]{3,2,1,0:T(2,128)S(1)}, f32[3,16,2,256]{3,2,1,0:T(2,128)S(1)}, u32[]{:S(2)}, u32[]{:S(2)}) collective-permute-start(f32[3,16,2,256]{3,2,1,0:T(2,128)S(1)} %get-tuple-element.31), channel_id=1, source_target_pairs={{0,1},{1,0},{2,3},{3,2},{4,5},{5,4},{6,7},{7,6},{8,9},{9,8},{10,11... | collective-permute-start | bytes 294920 | tf_op jit(solution)/shard_map/ppermute | solution.py:396
  31.8 8.2 %collective-permute-start.7 = (f32[3,16,2,256]{3,2,1,0:T(2,128)S(1)}, f32[3,16,2,256]{3,2,1,0:T(2,128)S(1)}, u32[]{:S(2)}, u32[]{:S(2)}) collective-permute-start(f32[3,16,2,256]{3,2,1,0:T(2,128)S(1)} %get-tuple-element.32), channel_id=1, source_target_pairs={{0,16},{1,2},{2,1},{3,4},{4,3},{5,6},{6,5},{7,8},{8,7},{9,10},{10,... | collective-permute-start | bytes 294920 | tf_op jit(solution)/shard_map/ppermute | solution.py:396
  35.5 4.6 %copy-start.3 = (f32[16,32,256]{2,1,0:T(8,128)S(1)}, f32[16,32,256]{2,1,0:T(8,128)}, u32[]{:S(2)}) copy-start(f32[16,32,256]{2,1,0:T(8,128)} %viscosity_ref.3) | copy-start | bytes 1572868

commit v4 on v3

--- a/solution.py
+++ b/solution.py
@@ -1,3 +1,5 @@
+import math
+
 import jax
 import jax.numpy as jnp
 from jax import lax
@@ -16,7 +18,8 @@
 GUESS_RATIO = 14.0
 ETAS = 32
 PIECES = 2
-UNROLL = 2
+UNROLL = 4
+TILE_ROWS = 3
 PACK_COST = 4_000_000_000
 FIELD_LANES = 64
 F32 = jnp.float32
@@ -139,8 +142,8 @@
         for x in range(nx):
             for y in range(0, ny, 8):
                 for h in range(nz // 128):
-                    start = ((h * nx + x) * ny + y) * 8 + c
-                    tiles[pl.ds(start, 8, stride=8), :] = field_ref[
+                    start = ((h * nx + x) * ny + y) * TILE_ROWS + c
+                    tiles[pl.ds(start, 8, stride=TILE_ROWS), :] = field_ref[
                         c, x, y : y + 8, 128 * h : 128 * h + 128
                     ]
     lane = lax.broadcasted_iota(jnp.int32, (8, 128), 1)
@@ -150,7 +153,7 @@
         for low in range(0, 128, 32):
             part = jnp.zeros((8, 128), F32)
             for spot in range(low, low + 32):
-                row = pl.multiple_of(rows_ref[start + spot], 8)
+                row = rows_ref[start + spot]
                 turned = pltpu.roll(tiles[pl.ds(row, 8), :], turns_ref[start + spot], 1)
                 part = jnp.where(lane == spot, turned, part)
             parts.append(part)
@@ -189,7 +192,7 @@
     tangent = [s - normal_part * n for s, n in zip(samples, normals)]
     speed = jnp.maximum(jnp.sqrt(sum(t * t for t in tangent)), SPEED_FLOOR)
     target = jnp.log(speed)
-    log_speed = target - jnp.log(jnp.full_like(target, GUESS_RATIO))
+    log_speed = target - math.log(GUESS_RATIO)
     index = row_iota((ETAS, points)).astype(F32)
     top = ETAS - 1.0
     eta = (index / top) * (index / top)
@@ -203,10 +206,11 @@
         fade = jnp.exp(-decay)
         damp = 1.0 - fade
         mixing = KAPPA * height * damp
-        share = weight / (NU_WALL + mixing * damp)
+        inverse = 1.0 / (NU_WALL + mixing * damp)
         growth = mixing * (damp + 2.0 * decay * fade)
+        share = weight * inverse
         total = jnp.sum(share, axis=0, keepdims=True)
-        change = jnp.sum(share * growth / (NU_WALL + mixing * damp), axis=0, keepdims=True)
+        change = jnp.sum(share * (growth * inverse), axis=0, keepdims=True)
         value = jnp.log(distance * pace * pace * total) - target
         log_speed = log_speed - value / (2.0 - change / total)
     stress = jnp.exp(2.0 * log_speed)
@@ -256,7 +260,7 @@
     _, nx, ny, nz = velocity_ref.shape
     cells = match_ref[...]
     half, row = (cells // 128) % (nz // 128), cells // nz
-    rows_ref[...] = (half * (nx * ny) + row) * 8
+    rows_ref[...] = (half * (nx * ny) + row) * TILE_ROWS
     turns_ref[...] = (lax.broadcasted_iota(jnp.int32, cells.shape, 1) - cells) & 127
     faces_of(velocity_ref, xa_ref, xb_ref, ya_ref, yb_ref)
 
@@ -321,8 +325,8 @@
         for k in range(4)
     ]
     distance = rows[0]
-    length = jnp.sqrt(rows[1] * rows[1] + rows[2] * rows[2] + rows[3] * rows[3])
-    normals = [row / length for row in rows[1:]]
+    inverse = 1.0 / jnp.sqrt(rows[1] * rows[1] + rows[2] * rows[2] + rows[3] * rows[3])
+    normals = [row * inverse for row in rows[1:]]
     geometry_ref[0:1, :] = distance
     for k in range(3):
         geometry_ref[k + 1 : k + 2, :] = normals[k]
@@ -427,7 +431,7 @@
     limit = pltpu.CompilerParams(vmem_limit_bytes=24 * 1024 * 1024)
     smem = pl.BlockSpec(memory_space=pltpu.SMEM)
     padded = pltpu.VMEM((comps, nz // 128, nx + 4, ny + 16, 128), F32)
-    tiles = pltpu.VMEM((8 * nx * ny * (nz // 128), 128), F32)
+    tiles = pltpu.VMEM((TILE_ROWS * nx * ny * (nz // 128) + 8, 128), F32)
 
     spots = jax.ShapeDtypeStruct(square, jnp.int32)
     outgoing = pl.pallas_call(
@@ -438,7 +442,7 @@
         compiler_params=limit,
         cost_estimate=pl.CostEstimate(flops=PACK_COST, bytes_accessed=98304, transcendentals=0),
         name="pack",
-    )(wall_geom)
+    )(pltpu.with_memory_space_constraint(wall_geom, pltpu.HBM))
     arrived = lax.all_to_all(
         outgoing.reshape(devices, 1, 128),
         ("region", "blk"), split_axis=0, concat_axis=0, tiled=True,

time: 43.8 us -> 44 us (level)
  the two profiles are of different devices: /device:TPU:24 before, /device:TPU:9 now
where the time goes in v4:
time: 44 us; the launch traced here: 43.6 us
  starting transfers between devices  18.7 us (42%)
  Pallas kernels  16.5 us (38%)
  local copies, waits for them, and re-layouts  6.28 us (14%)
  between operations  1.41 us (3%)
  waiting for transfers between devices  0.71 us (2%)
    ppermute x8, starting transfers between devices, swap(): return lax.ppermute(block, ('region', 'blk'), pairs)  11.2 us
    all_to_all x1, starting transfers between devices, local(): lax.all_to_all(outgoing.reshape(devices, 1, 128), ('region', 'blk'), spli...  7.49 us
    unnamed x22, local copies, waits for them, and re-layouts  6.28 us
    pallas_call x1, Pallas kernels, local(): pl.pallas_call(second_kernel, out_shape=(field, jax.ShapeDtypeStruct(squa...  4.2 us
    pallas_call x1, Pallas kernels, local(): pl.pallas_call(last_kernel, out_shape=field, in_specs=[vmem] * 7, out_spe...  3.31 us
    pallas_call x1, Pallas kernels, local(): pl.pallas_call(stress_kernel, out_shape=(field, xface, xface, yface, yfac...  2.7 us
    pallas_call x1, Pallas kernels, local(): pl.pallas_call(rate_kernel, out_shape=field, in_specs=[vmem] * 6, out_spe...  2.43 us
    pallas_call x1, Pallas kernels, local(): pl.pallas_call(sample_kernel, out_shape=(rowed, jax.ShapeDtypeStruct((1,...  2.1 us
  transfers between devices with their start and end apart: 9, of which 1 were waited for; matrix products, arithmetic and copies ran while one was open for 0% of the time, Pallas kernels for 24%

profile of v4, /device:TPU:9, one launch (start us, length us, event | category | flops | bytes accessed | tf_op | source)
XLA Modules:
  0.0 43.6 jit_solution(13908244641231277018)
XLA Ops:
  0.6 1.4 %copy-done = f32[3,16,32,256]{3,2,1,0:T(8,128)S(1)} copy-done((f32[3,16,32,256]{3,2,1,0:T(8,128)S(1)}, f32[3,16,32,256]{3,2,1,0:T(8,128)}, u32[]{:S(2)}) %copy-start) | copy-done | bytes 1572888
  2.0 0.7 %copy-done.10 = s32[1024]{0:T(1024)S(1)} copy-done((s32[1024]{0:T(1024)S(1)}, s32[1024]{0:T(1024)}, u32[]{:S(2)}) %copy-start.10) | copy-done | bytes 4120
  2.7 0.1 faces.1
  2.9 1.7 %collective-permute-start.2 = (f32[3,16,2,256]{3,2,1,0:T(2,128)S(1)}, f32[3,16,2,256]{3,2,1,0:T(2,128)S(1)}, u32[]{:S(2)}, u32[]{:S(2)}) collective-permute-start(f32[3,16,2,256]{3,2,1,0:T(2,128)S(1)} %get-tuple-element.24), channel_id=1, source_target_pairs={{0,1},{1,0},{2,3},{3,2},{4,5},{5,4},{6,7},{7,6},{8,9},{9,8},{10,11... | collective-permute-start | bytes 294920 | tf_op jit(solution)/shard_map/ppermute | solution.py:400
  4.6 2.1 %collective-permute-start.3 = (f32[3,16,2,256]{3,2,1,0:T(2,128)S(1)}, f32[3,16,2,256]{3,2,1,0:T(2,128)S(1)}, u32[]{:S(2)}, u32[]{:S(2)}) collective-permute-start(f32[3,16,2,256]{3,2,1,0:T(2,128)S(1)} %get-tuple-element.25), channel_id=1, source_target_pairs={{0,16},{1,2},{2,1},{3,4},{4,3},{5,6},{6,5},{7,8},{8,7},{9,10},{10,... | collective-permute-start | bytes 294920 | tf_op jit(solution)/shard_map/ppermute | solution.py:400
  6.7 1.2 %collective-permute-start = (f32[3,2,32,256]{3,2,1,0:T(8,128)S(1)}, f32[3,2,32,256]{3,2,1,0:T(8,128)S(1)}, u32[]{:S(2)}, u32[]{:S(2)}) collective-permute-start(f32[3,2,32,256]{3,2,1,0:T(8,128)S(1)} %get-tuple-element.22), channel_id=1, source_target_pairs={{0,16},{1,17},{2,18},{3,19},{4,20},{5,21},{6,22},{7,23},{8,24},{9,... | collective-permute-start | bytes 589832 | tf_op jit(solution)/shard_map/ppermute | solution.py:400
  7.9 1.1 %collective-permute-start.1 = (f32[3,2,32,256]{3,2,1,0:T(8,128)S(1)}, f32[3,2,32,256]{3,2,1,0:T(8,128)S(1)}, u32[]{:S(2)}, u32[]{:S(2)}) collective-permute-start(f32[3,2,32,256]{3,2,1,0:T(8,128)S(1)} %get-tuple-element.23), channel_id=1, source_target_pairs={{0,1},{1,0},{2,3},{3,2},{4,5},{5,4},{6,7},{7,6},{8,9},{9,8},{10,11... | collective-permute-start | bytes 589832 | tf_op jit(solution)/shard_map/ppermute | solution.py:400
  9.0 1.6 %pack.1 = f32[128,128]{1,0:T(8,128)} custom-call(f32[4,2048]{1,0:T(4,128)} %geometry_ref.1), custom_call_target="tpu_custom_call" | custom-call | flops 4000000000 | bytes 98304 | tf_op jit(solution)/shard_map/pack/pallas_call | solution.py:437
  10.7 7.5 %all-to-all-start = ((f32[128,1,128]{2,1,0:T(1,128)}), f32[128,1,128]{2,1,0:T(1,128)S(1)}, u32[]{:S(2)}, u32[]{:S(2)}) async-start(f32[128,1,128]{2,1,0:T(1,128)} %bitcast.1), calls=%async_computation | async-start | bytes 131072 | tf_op jit(solution)/shard_map/all_to_all | solution.py:446
  18.8 2.1 %sample.1 = (f32[4,1024]{1,0:T(4,128)S(1)}, f32[1,1024]{1,0:T(1,128)S(1)}) custom-call(s32[1024]{0:T(1024)S(1)} %bitcast.15, s32[1024]{0:T(1024)S(1)} %bitcast.17, f32[3,16,32,256]{3,2,1,0:T(8,128)S(1)} %copy-done.1, s32[8,128]{1,0:T(8,128)S(1)} %bitcast.11), custom_call_target="tpu_custom_call" | custom-call | tf_op jit(solution)/shard_map/sample/pallas_call | solution.py:460
  21.0 0.6 %copy-done.6 = f32[3,16,2,256]{3,2,1,0:T(2,128)} copy-done((f32[3,16,2,256]{3,2,1,0:T(2,128)}, f32[3,16,2,256]{3,2,1,0:T(2,128)S(1)}, u32[]{:S(2)}) %copy-start.6) | copy-done | bytes 98328
  21.6 0.7 %copy-done.4 = f32[3,2,32,256]{3,2,1,0:T(8,128)} copy-done((f32[3,2,32,256]{3,2,1,0:T(8,128)}, f32[3,2,32,256]{3,2,1,0:T(8,128)S(1)}, u32[]{:S(2)}) %copy-start.4) | copy-done | bytes 196632
  22.3 1.0 %copy-done.2 = f32[16,32,256]{2,1,0:T(8,128)S(1)} copy-done((f32[16,32,256]{2,1,0:T(8,128)S(1)}, f32[16,32,256]{2,1,0:T(8,128)}, u32[]{:S(2)}) %copy-start.2) | copy-done | bytes 524312
  23.3 0.9 %copy-done.5 = f32[3,2,32,256]{3,2,1,0:T(8,128)S(1)} copy-done((f32[3,2,32,256]{3,2,1,0:T(8,128)S(1)}, f32[3,2,32,256]{3,2,1,0:T(8,128)}, u32[]{:S(2)}) %copy-start.5) | copy-done | bytes 196632
  24.3 0.9 %copy-done.7 = f32[3,16,2,256]{3,2,1,0:T(2,128)S(1)} copy-done((f32[3,16,2,256]{3,2,1,0:T(2,128)S(1)}, f32[3,16,2,256]{3,2,1,0:T(2,128)}, u32[]{:S(2)}) %copy-start.7) | copy-done | bytes 98328
  25.1 2.4 %rate.1.base_ref = f32[3,16,32,256]{3,2,1,0:T(8,128)S(1)} custom-call(f32[3,16,32,256]{3,2,1,0:T(8,128)S(1)} %copy-done.1, f32[16,32,256]{2,1,0:T(8,128)S(1)} %copy-done.2, f32[3,2,32,256]{3,2,1,0:T(8,128)S(1)} %collective-permute-done.xa_ref, f32[3,2,32,256]{3,2,1,0:T(8,128)S(1)} %copy-done.5, f32[3,16,2,256]{3,2,1,0:T(2,128)S(1)} %collective-permute-done.2.ya_ref, ...), custom_call_target="tpu_custom_call" | custom-call | tf_op jit(solution)/shard_map/rate/pallas_call | solution.py:469
  27.6 2.7 %stress.1 = (f32[3,16,32,256]{3,2,1,0:T(8,128)S(1)}, f32[3,2,32,256]{3,2,1,0:T(8,128)S(1)}, f32[3,2,32,256]{3,2,1,0:T(8,128)S(1)}, f32[3,16,2,256]{3,2,1,0:T(2,1...) custom-call(s32[1]{0:T(128)S(6)} %copy.10.count_ref, f32[128,128]{1,0:T(8,128)S(1)} %bitcast.10, ...), custom_call_target="tpu_custom_call" | custom-call | tf_op jit(solution)/shard_map/stress/pallas_call | solution.py:478
  30.3 0.5 %collective-permute-start.4 = (f32[3,2,32,256]{3,2,1,0:T(8,128)S(1)}, f32[3,2,32,256]{3,2,1,0:T(8,128)S(1)}, u32[]{:S(2)}, u32[]{:S(2)}) collective-permute-start(f32[3,2,32,256]{3,2,1,0:T(8,128)S(1)} %get-tuple-element.29), channel_id=1, source_target_pairs={{0,16},{1,17},{2,18},{3,19},{4,20},{5,21},{6,22},{7,23},{8,24},{9,... | collective-permute-start | bytes 589832 | tf_op jit(solution)/shard_map/ppermute | solution.py:400
  30.8 1.2 %collective-permute-start.5 = (f32[3,2,32,256]{3,2,1,0:T(8,128)S(1)}, f32[3,2,32,256]{3,2,1,0:T(8,128)S(1)}, u32[]{:S(2)}, u32[]{:S(2)}) collective-permute-start(f32[3,2,32,256]{3,2,1,0:T(8,128)S(1)} %get-tuple-element.30), channel_id=1, source_target_pairs={{0,1},{1,0},{2,3},{3,2},{4,5},{5,4},{6,7},{7,6},{8,9},{9,8},{10,11... | collective-permute-start | bytes 589832 | tf_op jit(solution)/shard_map/ppermute | solution.py:400
  32.0 1.4 %collective-permute-start.6 = (f32[3,16,2,256]{3,2,1,0:T(2,128)S(1)}, f32[3,16,2,256]{3,2,1,0:T(2,128)S(1)}, u32[]{:S(2)}, u32[]{:S(2)}) collective-permute-start(f32[3,16,2,256]{3,2,1,0:T(2,128)S(1)} %get-tuple-element.31), channel_id=1, source_target_pairs={{0,1},{1,0},{2,3},{3,2},{4,5},{5,4},{6,7},{7,6},{8,9},{9,8},{10,11... | collective-permute-start | bytes 294920 | tf_op jit(solution)/shard_map/ppermute | solution.py:400
  33.4 2.0 %collective-permute-start.7 = (f32[3,16,2,256]{3,2,1,0:T(2,128)S(1)}, f32[3,16,2,256]{3,2,1,0:T(2,128)S(1)}, u32[]{:S(2)}, u32[]{:S(2)}) collective-permute-start(f32[3,16,2,256]{3,2,1,0:T(2,128)S(1)} %get-tuple-element.32), channel_id=1, source_target_pairs={{0,16},{1,2},{2,1},{3,4},{4,3},{5,6},{6,5},{7,8},{8,7},{9,10},{10,... | collective-permute-start | bytes 294920 | tf_op jit(solution)/shard_map/ppermute | solution.py:400
  35.3 4.2 %second.1 = (f32[3,16,32,256]{3,2,1,0:T(8,128)S(1)}, f32[8,128]{1,0:T(8,128)}) custom-call(s32[1]{0:T(128)S(6)} %copy.10.count_ref, s32[1024]{0:T(1024)S(1)} %bitcast.16, s32[1024]{0:T(1024)S(1)} %bitcast.18, f32[3,16,32,256]{3,2,1,0:T(8,128)S(1)} %copy-done.1, f32[3,16,32,256]{3,2,1,0:T(8,128)S(1)} %get-tuple-element.26.first_ref, s32[8,128]{1,0:T(8,128)S(1)} %bitcast.14, ...), custom_call_target="tpu_custom_call" | custom-call | tf_op jit(solution)/shard_map/second/pallas_call | solution.py:487
  39.6 0.7 %collective-permute-done.7.yb_ref = f32[3,16,2,256]{3,2,1,0:T(2,128)S(1)} collective-permute-done((f32[3,16,2,256]{3,2,1,0:T(2,128)S(1)}, f32[3,16,2,256]{3,2,1,0:T(2,128)S(1)}, u32[]{:S(2)}, u32[]{:S(2)}) %collective-permute-start.7) | collective-permute-done | bytes 98336 | tf_op jit(solution)/shard_map/ppermute | solution.py:400
  40.3 3.3 %last.1 = f32[3,16,32,256]{3,2,1,0:T(8,128)} custom-call(f32[16,32,256]{2,1,0:T(8,128)S(1)} %copy-done.3, f32[3,16,32,256]{3,2,1,0:T(8,128)S(1)} %get-tuple-element.26.first_ref, f32[3,16,32,256]{3,2,1,0:T(8,128)S(1)} %get-tuple-element.28.part_ref, f32[3,2,32,256]{3,2,1,0:T(8,128)S(1)} %collective-permute-done.4.xa_ref, ...), custom_call_target="tpu_custom_call" | custom-call | tf_op jit(solution)/shard_map/last/pallas_call | solution.py:496
  (23 shorter events, 0.1 us)
Async XLA Ops:
  0.6 1.4 %copy-start = (f32[3,16,32,256]{3,2,1,0:T(8,128)S(1)}, f32[3,16,32,256]{3,2,1,0:T(8,128)}, u32[]{:S(2)}) copy-start(f32[3,16,32,256]{3,2,1,0:T(8,128)} %velocity_ref.7) | copy-start | bytes 4718596
  2.0 0.7 %copy-start.10 = (s32[1024]{0:T(1024)S(1)}, s32[1024]{0:T(1024)}, u32[]{:S(2)}) copy-start(s32[1024]{0:T(1024)} %param.9) | copy-start | bytes 12292
  2.9 18.1 %collective-permute-start.2 = (f32[3,16,2,256]{3,2,1,0:T(2,128)S(1)}, f32[3,16,2,256]{3,2,1,0:T(2,128)S(1)}, u32[]{:S(2)}, u32[]{:S(2)}) collective-permute-start(f32[3,16,2,256]{3,2,1,0:T(2,128)S(1)} %get-tuple-element.24), channel_id=1, source_target_pairs={{0,1},{1,0},{2,3},{3,2},{4,5},{5,4},{6,7},{7,6},{8,9},{9,8},{10,11... | collective-permute-start | bytes 294920 | tf_op jit(solution)/shard_map/ppermute | solution.py:400
  4.6 16.4 %collective-permute-start.3 = (f32[3,16,2,256]{3,2,1,0:T(2,128)S(1)}, f32[3,16,2,256]{3,2,1,0:T(2,128)S(1)}, u32[]{:S(2)}, u32[]{:S(2)}) collective-permute-start(f32[3,16,2,256]{3,2,1,0:T(2,128)S(1)} %get-tuple-element.25), channel_id=1, source_target_pairs={{0,16},{1,2},{2,1},{3,4},{4,3},{5,6},{6,5},{7,8},{8,7},{9,10},{10,... | collective-permute-start | bytes 294920 | tf_op jit(solution)/shard_map/ppermute | solution.py:400
  6.7 14.9 %collective-permute-start = (f32[3,2,32,256]{3,2,1,0:T(8,128)S(1)}, f32[3,2,32,256]{3,2,1,0:T(8,128)S(1)}, u32[]{:S(2)}, u32[]{:S(2)}) collective-permute-start(f32[3,2,32,256]{3,2,1,0:T(8,128)S(1)} %get-tuple-element.22), channel_id=1, source_target_pairs={{0,16},{1,17},{2,18},{3,19},{4,20},{5,21},{6,22},{7,23},{8,24},{9,... | collective-permute-start | bytes 589832 | tf_op jit(solution)/shard_map/ppermute | solution.py:400
  7.9 10.9 %copy-start.1 = (f32[3,16,32,256]{3,2,1,0:T(8,128)S(1)}, f32[3,16,32,256]{3,2,1,0:T(8,128)}, u32[]{:S(2)}) copy-start(f32[3,16,32,256]{3,2,1,0:T(8,128)} %velocity_ref.7) | copy-start | bytes 4718596
  7.9 10.9 %copy-start.8 = (s32[1024,1]{0,1:T(1,128)S(1)}, s32[1024,1]{0,1:T(1,128)}, u32[]{:S(2)}) copy-start(s32[1024,1]{0,1:T(1,128)} %param.11) | copy-start | bytes 12292
  7.9 13.7 %collective-permute-start.1 = (f32[3,2,32,256]{3,2,1,0:T(8,128)S(1)}, f32[3,2,32,256]{3,2,1,0:T(8,128)S(1)}, u32[]{:S(2)}, u32[]{:S(2)}) collective-permute-start(f32[3,2,32,256]{3,2,1,0:T(8,128)S(1)} %get-tuple-element.23), channel_id=1, source_target_pairs={{0,1},{1,0},{2,3},{3,2},{4,5},{5,4},{6,7},{7,6},{8,9},{9,8},{10,11... | collective-permute-start | bytes 589832 | tf_op jit(solution)/shard_map/ppermute | solution.py:400
  10.7 16.9 %all-to-all-start = ((f32[128,1,128]{2,1,0:T(1,128)}), f32[128,1,128]{2,1,0:T(1,128)S(1)}, u32[]{:S(2)}, u32[]{:S(2)}) async-start(f32[128,1,128]{2,1,0:T(1,128)} %bitcast.1), calls=%async_computation | async-start | bytes 131072 | tf_op jit(solution)/shard_map/all_to_all | solution.py:446
  18.8 8.8 %copy-start.9 = (s32[1024]{0:T(1024)S(1)}, s32[1024]{0:T(1024)}, u32[]{:S(2)}) copy-start(s32[1024]{0:T(1024)} %param.10) | copy-start | bytes 12292
  21.0 0.6 %copy-start.6 = (f32[3,16,2,256]{3,2,1,0:T(2,128)}, f32[3,16,2,256]{3,2,1,0:T(2,128)S(1)}, u32[]{:S(2)}) copy-start(f32[3,16,2,256]{3,2,1,0:T(2,128)S(1)} %collective-permute-done.3.yb_ref) | copy-start | bytes 294916
  21.6 0.7 %copy-start.4 = (f32[3,2,32,256]{3,2,1,0:T(8,128)}, f32[3,2,32,256]{3,2,1,0:T(8,128)S(1)}, u32[]{:S(2)}) copy-start(f32[3,2,32,256]{3,2,1,0:T(8,128)S(1)} %collective-permute-done.1.xb_ref) | copy-start | bytes 589828
  22.3 1.0 %copy-start.2 = (f32[16,32,256]{2,1,0:T(8,128)S(1)}, f32[16,32,256]{2,1,0:T(8,128)}, u32[]{:S(2)}) copy-start(f32[16,32,256]{2,1,0:T(8,128)} %viscosity_ref.3) | copy-start | bytes 1572868
  23.3 0.9 %copy-start.5 = (f32[3,2,32,256]{3,2,1,0:T(8,128)S(1)}, f32[3,2,32,256]{3,2,1,0:T(8,128)}, u32[]{:S(2)}) copy-start(f32[3,2,32,256]{3,2,1,0:T(8,128)} %copy-done.4) | copy-start | bytes 589828
  24.3 0.9 %copy-start.7 = (f32[3,16,2,256]{3,2,1,0:T(2,128)S(1)}, f32[3,16,2,256]{3,2,1,0:T(2,128)}, u32[]{:S(2)}) copy-start(f32[3,16,2,256]{3,2,1,0:T(2,128)} %copy-done.6) | copy-start | bytes 294916
  30.3 10.0 %collective-permute-start.4 = (f32[3,2,32,256]{3,2,1,0:T(8,128)S(1)}, f32[3,2,32,256]{3,2,1,0:T(8,128)S(1)}, u32[]{:S(2)}, u32[]{:S(2)}) collective-permute-start(f32[3,2,32,256]{3,2,1,0:T(8,128)S(1)} %get-tuple-element.29), channel_id=1, source_target_pairs={{0,16},{1,17},{2,18},{3,19},{4,20},{5,21},{6,22},{7,23},{8,24},{9,... | collective-permute-start | bytes 589832 | tf_op jit(solution)/shard_map/ppermute | solution.py:400
  30.8 9.5 %collective-permute-start.5 = (f32[3,2,32,256]{3,2,1,0:T(8,128)S(1)}, f32[3,2,32,256]{3,2,1,0:T(8,128)S(1)}, u32[]{:S(2)}, u32[]{:S(2)}) collective-permute-start(f32[3,2,32,256]{3,2,1,0:T(8,128)S(1)} %get-tuple-element.30), channel_id=1, source_target_pairs={{0,1},{1,0},{2,3},{3,2},{4,5},{5,4},{6,7},{7,6},{8,9},{9,8},{10,11... | collective-permute-start | bytes 589832 | tf_op jit(solution)/shard_map/ppermute | solution.py:400
  32.0 7.6 %collective-permute-start.6 = (f32[3,16,2,256]{3,2,1,0:T(2,128)S(1)}, f32[3,16,2,256]{3,2,1,0:T(2,128)S(1)}, u32[]{:S(2)}, u32[]{:S(2)}) collective-permute-start(f32[3,16,2,256]{3,2,1,0:T(2,128)S(1)} %get-tuple-element.31), channel_id=1, source_target_pairs={{0,1},{1,0},{2,3},{3,2},{4,5},{5,4},{6,7},{7,6},{8,9},{9,8},{10,11... | collective-permute-start | bytes 294920 | tf_op jit(solution)/shard_map/ppermute | solution.py:400
  33.4 6.9 %collective-permute-start.7 = (f32[3,16,2,256]{3,2,1,0:T(2,128)S(1)}, f32[3,16,2,256]{3,2,1,0:T(2,128)S(1)}, u32[]{:S(2)}, u32[]{:S(2)}) collective-permute-start(f32[3,16,2,256]{3,2,1,0:T(2,128)S(1)} %get-tuple-element.32), channel_id=1, source_target_pairs={{0,16},{1,2},{2,1},{3,4},{4,3},{5,6},{6,5},{7,8},{8,7},{9,10},{10,... | collective-permute-start | bytes 294920 | tf_op jit(solution)/shard_map/ppermute | solution.py:400
  35.3 4.9 %copy-start.3 = (f32[16,32,256]{2,1,0:T(8,128)S(1)}, f32[16,32,256]{2,1,0:T(8,128)}, u32[]{:S(2)}) copy-start(f32[16,32,256]{2,1,0:T(8,128)} %viscosity_ref.3) | copy-start | bytes 1572868

commit v5 on v4

--- a/solution.py
+++ b/solution.py
@@ -136,7 +136,7 @@
     lax.fori_loop(0, nx, plane, 0, unroll=UNROLL)
 
 
-def sample_at(field_ref, rows_ref, turns_ref, tiles):
+def lay_tiles(field_ref, tiles):
     comps, nx, ny, nz = field_ref.shape
     for c in range(comps):
         for x in range(nx):
@@ -146,6 +146,9 @@
                     tiles[pl.ds(start, 8, stride=TILE_ROWS), :] = field_ref[
                         c, x, y : y + 8, 128 * h : 128 * h + 128
                     ]
+
+
+def sample_at(tiles, comps, rows_ref, turns_ref):
     lane = lax.broadcasted_iota(jnp.int32, (8, 128), 1)
     blocks = []
     for start in range(0, rows_ref.shape[0], 128):
@@ -220,7 +223,8 @@
 
 def sample_kernel(rows_ref, turns_ref, velocity_ref, dest_ref, samples_ref, rank_ref, tiles):
     points = rows_ref.shape[0]
-    samples = sample_at(velocity_ref, rows_ref, turns_ref, tiles)
+    lay_tiles(velocity_ref, tiles)
+    samples = sample_at(tiles, velocity_ref.shape[0], rows_ref, turns_ref)
     for c in range(3):
         samples_ref[c : c + 1, :] = samples[c]
     owners = as_row(dest_ref[...])
@@ -301,7 +305,7 @@
 
 def stress_kernel(
     count_ref, arrived_ref, dest_ref, wall_ref, rank_ref, samples_ref, base_ref,
-    first_ref, xa_ref, xb_ref, ya_ref, yb_ref, geometry_ref,
+    first_ref, xa_ref, xb_ref, ya_ref, yb_ref, geometry_ref, tiles,
 ):
     comps, nx, ny, nz = base_ref.shape
     devices = arrived_ref.shape[0]
@@ -339,15 +343,16 @@
         block = force[:, c * nz : (c + 1) * nz] * (TIME_STEP / WALL_DY)
         first_ref[c] = base_ref[c] + block.reshape(nx, ny, nz)
     faces_of(first_ref, xa_ref, xb_ref, ya_ref, yb_ref)
+    lay_tiles(first_ref, tiles)
 
 
 def second_kernel(
-    count_ref, rows_ref, turns_ref, velocity_ref, first_ref, wall_ref, geometry_ref,
-    part_ref, log_ref, tiles,
+    count_ref, rows_ref, turns_ref, velocity_ref, tiles, wall_ref, geometry_ref,
+    part_ref, log_ref,
 ):
-    comps, nx, ny, nz = first_ref.shape
+    comps, nx, ny, nz = velocity_ref.shape
     points = rows_ref.shape[0]
-    samples = sample_at(first_ref, rows_ref, turns_ref, tiles)
+    samples = sample_at(tiles, comps, rows_ref, turns_ref)
     distance = geometry_ref[0:1, :]
     normals = [geometry_ref[k : k + 1, :] for k in range(1, 4)]
     stress, log_stress = wall_solve(samples, distance, normals)
@@ -356,7 +361,7 @@
     for i in range(log_ref.shape[0]):
         log_ref[i : i + 1, :] = log_stress[:, i * 128 : (i + 1) * 128]
     stress = [jnp.where(live, value, 0.0) for value in stress]
-    force = scatter_sum(stress, as_row(wall_ref[...]), live, first_ref.shape)
+    force = scatter_sum(stress, as_row(wall_ref[...]), live, velocity_ref.shape)
     for c in range(comps):
         block = force[:, c * nz : (c + 1) * nz] * (0.5 * TIME_STEP / WALL_DY)
         part_ref[c] = 0.5 * velocity_ref[c] + block.reshape(nx, ny, nz)
@@ -475,11 +480,14 @@
         compiler_params=limit,
         name="rate",
     )(velocity, viscosity, *halos)
-    first, *faces, geometry = pl.pallas_call(
+    first, *faces, geometry, laid = pl.pallas_call(
         stress_kernel,
-        out_shape=(field, xface, xface, yface, yface, rowed),
+        out_shape=(
+            field, xface, xface, yface, yface, rowed,
+            jax.ShapeDtypeStruct(tiles.shape, F32),
+        ),
         in_specs=[smem] + [vmem] * 6,
-        out_specs=(vmem,) * 6,
+        out_specs=(vmem,) * 7,
         compiler_params=limit,
         name="stress",
     )(match_count, arrived, dest, wall, rank, samples, base)
@@ -489,10 +497,9 @@
         out_shape=(field, jax.ShapeDtypeStruct(square, F32)),
         in_specs=[smem] * 3 + [vmem] * 4,
         out_specs=(vmem,) * 2,
-        scratch_shapes=[tiles],
         compiler_params=limit,
         name="second",
-    )(match_count, rows, turns, velocity, first, wall, geometry)
+    )(match_count, rows, turns, velocity, laid, wall, geometry)
     advanced = pl.pallas_call(
         last_kernel,
         out_shape=field,

time: 44 us -> 44 us (level)
  no operation moved by 1% of the time
where the time goes in v5:
time: 44 us; the launch traced here: 43.6 us
  starting transfers between devices  18.7 us (42%)
  Pallas kernels  16.4 us (37%)
  local copies, waits for them, and re-layouts  6.28 us (14%)
  between operations  1.41 us (3%)
  waiting for transfers between devices  0.79 us (2%)
    ppermute x8, starting transfers between devices, swap(): return lax.ppermute(block, ('region', 'blk'), pairs)  11.2 us
    all_to_all x1, starting transfers between devices, local(): lax.all_to_all(outgoing.reshape(devices, 1, 128), ('region', 'blk'), spli...  7.49 us
    unnamed x22, local copies, waits for them, and re-layouts  6.28 us
    pallas_call x1, Pallas kernels, local(): pl.pallas_call(second_kernel, out_shape=(field, jax.ShapeDtypeStruct(squa...  4.11 us
    pallas_call x1, Pallas kernels, local(): pl.pallas_call(last_kernel, out_shape=field, in_specs=[vmem] * 7, out_spe...  3.32 us
    pallas_call x1, Pallas kernels, local(): pl.pallas_call(stress_kernel, out_shape=(field, xface, xface, yface, yfac...  2.71 us
    pallas_call x1, Pallas kernels, local(): pl.pallas_call(rate_kernel, out_shape=field, in_specs=[vmem] * 6, out_spe...  2.43 us
    pallas_call x1, Pallas kernels, local(): pl.pallas_call(sample_kernel, out_shape=(rowed, jax.ShapeDtypeStruct((1,...  2.1 us
  transfers between devices with their start and end apart: 9, of which 1 were waited for; matrix products, arithmetic and copies ran while one was open for 0% of the time, Pallas kernels for 24%

profile of v5, /device:TPU:9, one launch (start us, length us, event | category | flops | bytes accessed | tf_op | source)
XLA Modules:
  0.0 43.6 jit_solution(17529430129471912563)
XLA Ops:
  0.6 1.4 %copy-done = f32[3,16,32,256]{3,2,1,0:T(8,128)S(1)} copy-done((f32[3,16,32,256]{3,2,1,0:T(8,128)S(1)}, f32[3,16,32,256]{3,2,1,0:T(8,128)}, u32[]{:S(2)}) %copy-start) | copy-done | bytes 1572888
  2.0 0.7 %copy-done.10 = s32[1024]{0:T(1024)S(1)} copy-done((s32[1024]{0:T(1024)S(1)}, s32[1024]{0:T(1024)}, u32[]{:S(2)}) %copy-start.10) | copy-done | bytes 4120
  2.7 0.1 faces.1
  2.9 1.7 %collective-permute-start.2 = (f32[3,16,2,256]{3,2,1,0:T(2,128)S(1)}, f32[3,16,2,256]{3,2,1,0:T(2,128)S(1)}, u32[]{:S(2)}, u32[]{:S(2)}) collective-permute-start(f32[3,16,2,256]{3,2,1,0:T(2,128)S(1)} %get-tuple-element.25), channel_id=1, source_target_pairs={{0,1},{1,0},{2,3},{3,2},{4,5},{5,4},{6,7},{7,6},{8,9},{9,8},{10,11... | collective-permute-start | bytes 294920 | tf_op jit(solution)/shard_map/ppermute | solution.py:405
  4.6 2.1 %collective-permute-start.3 = (f32[3,16,2,256]{3,2,1,0:T(2,128)S(1)}, f32[3,16,2,256]{3,2,1,0:T(2,128)S(1)}, u32[]{:S(2)}, u32[]{:S(2)}) collective-permute-start(f32[3,16,2,256]{3,2,1,0:T(2,128)S(1)} %get-tuple-element.26), channel_id=1, source_target_pairs={{0,16},{1,2},{2,1},{3,4},{4,3},{5,6},{6,5},{7,8},{8,7},{9,10},{10,... | collective-permute-start | bytes 294920 | tf_op jit(solution)/shard_map/ppermute | solution.py:405
  6.7 1.2 %collective-permute-start = (f32[3,2,32,256]{3,2,1,0:T(8,128)S(1)}, f32[3,2,32,256]{3,2,1,0:T(8,128)S(1)}, u32[]{:S(2)}, u32[]{:S(2)}) collective-permute-start(f32[3,2,32,256]{3,2,1,0:T(8,128)S(1)} %get-tuple-element.23), channel_id=1, source_target_pairs={{0,16},{1,17},{2,18},{3,19},{4,20},{5,21},{6,22},{7,23},{8,24},{9,... | collective-permute-start | bytes 589832 | tf_op jit(solution)/shard_map/ppermute | solution.py:405
  7.9 1.1 %collective-permute-start.1 = (f32[3,2,32,256]{3,2,1,0:T(8,128)S(1)}, f32[3,2,32,256]{3,2,1,0:T(8,128)S(1)}, u32[]{:S(2)}, u32[]{:S(2)}) collective-permute-start(f32[3,2,32,256]{3,2,1,0:T(8,128)S(1)} %get-tuple-element.24), channel_id=1, source_target_pairs={{0,1},{1,0},{2,3},{3,2},{4,5},{5,4},{6,7},{7,6},{8,9},{9,8},{10,11... | collective-permute-start | bytes 589832 | tf_op jit(solution)/shard_map/ppermute | solution.py:405
  9.0 1.6 %pack.1 = f32[128,128]{1,0:T(8,128)} custom-call(f32[4,2048]{1,0:T(4,128)} %geometry_ref.1), custom_call_target="tpu_custom_call" | custom-call | flops 4000000000 | bytes 98304 | tf_op jit(solution)/shard_map/pack/pallas_call | solution.py:442
  10.7 7.5 %all-to-all-start = ((f32[128,1,128]{2,1,0:T(1,128)}), f32[128,1,128]{2,1,0:T(1,128)S(1)}, u32[]{:S(2)}, u32[]{:S(2)}) async-start(f32[128,1,128]{2,1,0:T(1,128)} %bitcast.1), calls=%async_computation | async-start | bytes 131072 | tf_op jit(solution)/shard_map/all_to_all | solution.py:451
  18.8 2.1 %sample.1 = (f32[4,1024]{1,0:T(4,128)S(1)}, f32[1,1024]{1,0:T(1,128)S(1)}) custom-call(s32[1024]{0:T(1024)S(1)} %bitcast.15, s32[1024]{0:T(1024)S(1)} %bitcast.17, f32[3,16,32,256]{3,2,1,0:T(8,128)S(1)} %copy-done.1, s32[8,128]{1,0:T(8,128)S(1)} %bitcast.11), custom_call_target="tpu_custom_call" | custom-call | tf_op jit(solution)/shard_map/sample/pallas_call | solution.py:465
  21.0 0.6 %copy-done.6 = f32[3,16,2,256]{3,2,1,0:T(2,128)} copy-done((f32[3,16,2,256]{3,2,1,0:T(2,128)}, f32[3,16,2,256]{3,2,1,0:T(2,128)S(1)}, u32[]{:S(2)}) %copy-start.6) | copy-done | bytes 98328
  21.6 0.7 %copy-done.4 = f32[3,2,32,256]{3,2,1,0:T(8,128)} copy-done((f32[3,2,32,256]{3,2,1,0:T(8,128)}, f32[3,2,32,256]{3,2,1,0:T(8,128)S(1)}, u32[]{:S(2)}) %copy-start.4) | copy-done | bytes 196632
  22.3 1.0 %copy-done.2 = f32[16,32,256]{2,1,0:T(8,128)S(1)} copy-done((f32[16,32,256]{2,1,0:T(8,128)S(1)}, f32[16,32,256]{2,1,0:T(8,128)}, u32[]{:S(2)}) %copy-start.2) | copy-done | bytes 524312
  23.3 0.9 %copy-done.5 = f32[3,2,32,256]{3,2,1,0:T(8,128)S(1)} copy-done((f32[3,2,32,256]{3,2,1,0:T(8,128)S(1)}, f32[3,2,32,256]{3,2,1,0:T(8,128)}, u32[]{:S(2)}) %copy-start.5) | copy-done | bytes 196632
  24.3 0.9 %copy-done.7 = f32[3,16,2,256]{3,2,1,0:T(2,128)S(1)} copy-done((f32[3,16,2,256]{3,2,1,0:T(2,128)S(1)}, f32[3,16,2,256]{3,2,1,0:T(2,128)}, u32[]{:S(2)}) %copy-start.7) | copy-done | bytes 98328
  25.1 2.4 %rate.1.base_ref = f32[3,16,32,256]{3,2,1,0:T(8,128)S(1)} custom-call(f32[3,16,32,256]{3,2,1,0:T(8,128)S(1)} %copy-done.1, f32[16,32,256]{2,1,0:T(8,128)S(1)} %copy-done.2, f32[3,2,32,256]{3,2,1,0:T(8,128)S(1)} %collective-permute-done.xa_ref, f32[3,2,32,256]{3,2,1,0:T(8,128)S(1)} %copy-done.5, f32[3,16,2,256]{3,2,1,0:T(2,128)S(1)} %collective-permute-done.2.ya_ref, ...), custom_call_target="tpu_custom_call" | custom-call | tf_op jit(solution)/shard_map/rate/pallas_call | solution.py:474
  27.6 2.7 %stress.1 = (f32[3,16,32,256]{3,2,1,0:T(8,128)S(1)}, f32[3,2,32,256]{3,2,1,0:T(8,128)S(1)}, f32[3,2,32,256]{3,2,1,0:T(8,128)S(1)}, f32[3,16,2,256]{3,2,1,0:T(2,1...) custom-call(s32[1]{0:T(128)S(6)} %copy.10.count_ref, ...), custom_call_target="tpu_custom_call" | custom-call | tf_op jit(solution)/shard_map/stress/pallas_call | solution.py:483
  30.3 0.5 %collective-permute-start.4 = (f32[3,2,32,256]{3,2,1,0:T(8,128)S(1)}, f32[3,2,32,256]{3,2,1,0:T(8,128)S(1)}, u32[]{:S(2)}, u32[]{:S(2)}) collective-permute-start(f32[3,2,32,256]{3,2,1,0:T(8,128)S(1)} %get-tuple-element.31), channel_id=1, source_target_pairs={{0,16},{1,17},{2,18},{3,19},{4,20},{5,21},{6,22},{7,23},{8,24},{9,... | collective-permute-start | bytes 589832 | tf_op jit(solution)/shard_map/ppermute | solution.py:405
  30.8 1.2 %collective-permute-start.5 = (f32[3,2,32,256]{3,2,1,0:T(8,128)S(1)}, f32[3,2,32,256]{3,2,1,0:T(8,128)S(1)}, u32[]{:S(2)}, u32[]{:S(2)}) collective-permute-start(f32[3,2,32,256]{3,2,1,0:T(8,128)S(1)} %get-tuple-element.32), channel_id=1, source_target_pairs={{0,1},{1,0},{2,3},{3,2},{4,5},{5,4},{6,7},{7,6},{8,9},{9,8},{10,11... | collective-permute-start | bytes 589832 | tf_op jit(solution)/shard_map/ppermute | solution.py:405
  32.0 1.4 %collective-permute-start.6 = (f32[3,16,2,256]{3,2,1,0:T(2,128)S(1)}, f32[3,16,2,256]{3,2,1,0:T(2,128)S(1)}, u32[]{:S(2)}, u32[]{:S(2)}) collective-permute-start(f32[3,16,2,256]{3,2,1,0:T(2,128)S(1)} %get-tuple-element.33), channel_id=1, source_target_pairs={{0,1},{1,0},{2,3},{3,2},{4,5},{5,4},{6,7},{7,6},{8,9},{9,8},{10,11... | collective-permute-start | bytes 294920 | tf_op jit(solution)/shard_map/ppermute | solution.py:405
  33.4 2.0 %collective-permute-start.7 = (f32[3,16,2,256]{3,2,1,0:T(2,128)S(1)}, f32[3,16,2,256]{3,2,1,0:T(2,128)S(1)}, u32[]{:S(2)}, u32[]{:S(2)}) collective-permute-start(f32[3,16,2,256]{3,2,1,0:T(2,128)S(1)} %get-tuple-element.34), channel_id=1, source_target_pairs={{0,16},{1,2},{2,1},{3,4},{4,3},{5,6},{6,5},{7,8},{8,7},{9,10},{10,... | collective-permute-start | bytes 294920 | tf_op jit(solution)/shard_map/ppermute | solution.py:405
  35.4 4.1 %second.1 = (f32[3,16,32,256]{3,2,1,0:T(8,128)S(1)}, f32[8,128]{1,0:T(8,128)}) custom-call(s32[1]{0:T(128)S(6)} %copy.10.count_ref, s32[1024]{0:T(1024)S(1)} %bitcast.16, s32[1024]{0:T(1024)S(1)} %bitcast.18, f32[3,16,32,256]{3,2,1,0:T(8,128)S(1)} %copy-done.1, f32[3080,128]{1,0:T(8,128)S(1)} %get-tuple-element.28.tiles, s32[8,128]{1,0:T(8,128)S(1)} %bitcast.14, ...), custom_call_target="tpu_custom_call" | custom-call | tf_op jit(solution)/shard_map/second/pallas_call | solution.py:495
  39.5 0.8 %collective-permute-done.7.yb_ref = f32[3,16,2,256]{3,2,1,0:T(2,128)S(1)} collective-permute-done((f32[3,16,2,256]{3,2,1,0:T(2,128)S(1)}, f32[3,16,2,256]{3,2,1,0:T(2,128)S(1)}, u32[]{:S(2)}, u32[]{:S(2)}) %collective-permute-start.7) | collective-permute-done | bytes 98336 | tf_op jit(solution)/shard_map/ppermute | solution.py:405
  40.3 3.3 %last.1 = f32[3,16,32,256]{3,2,1,0:T(8,128)} custom-call(f32[16,32,256]{2,1,0:T(8,128)S(1)} %copy-done.3, f32[3,16,32,256]{3,2,1,0:T(8,128)S(1)} %get-tuple-element.27.first_ref, f32[3,16,32,256]{3,2,1,0:T(8,128)S(1)} %get-tuple-element.30.part_ref, f32[3,2,32,256]{3,2,1,0:T(8,128)S(1)} %collective-permute-done.4.xa_ref, ...), custom_call_target="tpu_custom_call" | custom-call | tf_op jit(solution)/shard_map/last/pallas_call | solution.py:503
  (23 shorter events, 0.1 us)
Async XLA Ops:
  0.6 1.4 %copy-start = (f32[3,16,32,256]{3,2,1,0:T(8,128)S(1)}, f32[3,16,32,256]{3,2,1,0:T(8,128)}, u32[]{:S(2)}) copy-start(f32[3,16,32,256]{3,2,1,0:T(8,128)} %velocity_ref.7) | copy-start | bytes 4718596
  2.0 0.7 %copy-start.10 = (s32[1024]{0:T(1024)S(1)}, s32[1024]{0:T(1024)}, u32[]{:S(2)}) copy-start(s32[1024]{0:T(1024)} %param.9) | copy-start | bytes 12292
  2.9 18.1 %collective-permute-start.2 = (f32[3,16,2,256]{3,2,1,0:T(2,128)S(1)}, f32[3,16,2,256]{3,2,1,0:T(2,128)S(1)}, u32[]{:S(2)}, u32[]{:S(2)}) collective-permute-start(f32[3,16,2,256]{3,2,1,0:T(2,128)S(1)} %get-tuple-element.25), channel_id=1, source_target_pairs={{0,1},{1,0},{2,3},{3,2},{4,5},{5,4},{6,7},{7,6},{8,9},{9,8},{10,11... | collective-permute-start | bytes 294920 | tf_op jit(solution)/shard_map/ppermute | solution.py:405
  4.6 16.4 %collective-permute-start.3 = (f32[3,16,2,256]{3,2,1,0:T(2,128)S(1)}, f32[3,16,2,256]{3,2,1,0:T(2,128)S(1)}, u32[]{:S(2)}, u32[]{:S(2)}) collective-permute-start(f32[3,16,2,256]{3,2,1,0:T(2,128)S(1)} %get-tuple-element.26), channel_id=1, source_target_pairs={{0,16},{1,2},{2,1},{3,4},{4,3},{5,6},{6,5},{7,8},{8,7},{9,10},{10,... | collective-permute-start | bytes 294920 | tf_op jit(solution)/shard_map/ppermute | solution.py:405
  6.7 14.9 %collective-permute-start = (f32[3,2,32,256]{3,2,1,0:T(8,128)S(1)}, f32[3,2,32,256]{3,2,1,0:T(8,128)S(1)}, u32[]{:S(2)}, u32[]{:S(2)}) collective-permute-start(f32[3,2,32,256]{3,2,1,0:T(8,128)S(1)} %get-tuple-element.23), channel_id=1, source_target_pairs={{0,16},{1,17},{2,18},{3,19},{4,20},{5,21},{6,22},{7,23},{8,24},{9,... | collective-permute-start | bytes 589832 | tf_op jit(solution)/shard_map/ppermute | solution.py:405
  7.9 10.9 %copy-start.1 = (f32[3,16,32,256]{3,2,1,0:T(8,128)S(1)}, f32[3,16,32,256]{3,2,1,0:T(8,128)}, u32[]{:S(2)}) copy-start(f32[3,16,32,256]{3,2,1,0:T(8,128)} %velocity_ref.7) | copy-start | bytes 4718596
  7.9 10.9 %copy-start.8 = (s32[1024,1]{0,1:T(1,128)S(1)}, s32[1024,1]{0,1:T(1,128)}, u32[]{:S(2)}) copy-start(s32[1024,1]{0,1:T(1,128)} %param.11) | copy-start | bytes 12292
  7.9 13.7 %collective-permute-start.1 = (f32[3,2,32,256]{3,2,1,0:T(8,128)S(1)}, f32[3,2,32,256]{3,2,1,0:T(8,128)S(1)}, u32[]{:S(2)}, u32[]{:S(2)}) collective-permute-start(f32[3,2,32,256]{3,2,1,0:T(8,128)S(1)} %get-tuple-element.24), channel_id=1, source_target_pairs={{0,1},{1,0},{2,3},{3,2},{4,5},{5,4},{6,7},{7,6},{8,9},{9,8},{10,11... | collective-permute-start | bytes 589832 | tf_op jit(solution)/shard_map/ppermute | solution.py:405
  10.7 16.9 %all-to-all-start = ((f32[128,1,128]{2,1,0:T(1,128)}), f32[128,1,128]{2,1,0:T(1,128)S(1)}, u32[]{:S(2)}, u32[]{:S(2)}) async-start(f32[128,1,128]{2,1,0:T(1,128)} %bitcast.1), calls=%async_computation | async-start | bytes 131072 | tf_op jit(solution)/shard_map/all_to_all | solution.py:451
  18.8 8.8 %copy-start.9 = (s32[1024]{0:T(1024)S(1)}, s32[1024]{0:T(1024)}, u32[]{:S(2)}) copy-start(s32[1024]{0:T(1024)} %param.10) | copy-start | bytes 12292
  21.0 0.6 %copy-start.6 = (f32[3,16,2,256]{3,2,1,0:T(2,128)}, f32[3,16,2,256]{3,2,1,0:T(2,128)S(1)}, u32[]{:S(2)}) copy-start(f32[3,16,2,256]{3,2,1,0:T(2,128)S(1)} %collective-permute-done.3.yb_ref) | copy-start | bytes 294916
  21.6 0.7 %copy-start.4 = (f32[3,2,32,256]{3,2,1,0:T(8,128)}, f32[3,2,32,256]{3,2,1,0:T(8,128)S(1)}, u32[]{:S(2)}) copy-start(f32[3,2,32,256]{3,2,1,0:T(8,128)S(1)} %collective-permute-done.1.xb_ref) | copy-start | bytes 589828
  22.3 1.0 %copy-start.2 = (f32[16,32,256]{2,1,0:T(8,128)S(1)}, f32[16,32,256]{2,1,0:T(8,128)}, u32[]{:S(2)}) copy-start(f32[16,32,256]{2,1,0:T(8,128)} %viscosity_ref.3) | copy-start | bytes 1572868
  23.3 0.9 %copy-start.5 = (f32[3,2,32,256]{3,2,1,0:T(8,128)S(1)}, f32[3,2,32,256]{3,2,1,0:T(8,128)}, u32[]{:S(2)}) copy-start(f32[3,2,32,256]{3,2,1,0:T(8,128)} %copy-done.4) | copy-start | bytes 589828
  24.3 0.9 %copy-start.7 = (f32[3,16,2,256]{3,2,1,0:T(2,128)S(1)}, f32[3,16,2,256]{3,2,1,0:T(2,128)}, u32[]{:S(2)}) copy-start(f32[3,16,2,256]{3,2,1,0:T(2,128)} %copy-done.6) | copy-start | bytes 294916
  30.3 10.0 %collective-permute-start.4 = (f32[3,2,32,256]{3,2,1,0:T(8,128)S(1)}, f32[3,2,32,256]{3,2,1,0:T(8,128)S(1)}, u32[]{:S(2)}, u32[]{:S(2)}) collective-permute-start(f32[3,2,32,256]{3,2,1,0:T(8,128)S(1)} %get-tuple-element.31), channel_id=1, source_target_pairs={{0,16},{1,17},{2,18},{3,19},{4,20},{5,21},{6,22},{7,23},{8,24},{9,... | collective-permute-start | bytes 589832 | tf_op jit(solution)/shard_map/ppermute | solution.py:405
  30.8 9.5 %collective-permute-start.5 = (f32[3,2,32,256]{3,2,1,0:T(8,128)S(1)}, f32[3,2,32,256]{3,2,1,0:T(8,128)S(1)}, u32[]{:S(2)}, u32[]{:S(2)}) collective-permute-start(f32[3,2,32,256]{3,2,1,0:T(8,128)S(1)} %get-tuple-element.32), channel_id=1, source_target_pairs={{0,1},{1,0},{2,3},{3,2},{4,5},{5,4},{6,7},{7,6},{8,9},{9,8},{10,11... | collective-permute-start | bytes 589832 | tf_op jit(solution)/shard_map/ppermute | solution.py:405
  32.0 7.5 %collective-permute-start.6 = (f32[3,16,2,256]{3,2,1,0:T(2,128)S(1)}, f32[3,16,2,256]{3,2,1,0:T(2,128)S(1)}, u32[]{:S(2)}, u32[]{:S(2)}) collective-permute-start(f32[3,16,2,256]{3,2,1,0:T(2,128)S(1)} %get-tuple-element.33), channel_id=1, source_target_pairs={{0,1},{1,0},{2,3},{3,2},{4,5},{5,4},{6,7},{7,6},{8,9},{9,8},{10,11... | collective-permute-start | bytes 294920 | tf_op jit(solution)/shard_map/ppermute | solution.py:405
  33.4 6.9 %collective-permute-start.7 = (f32[3,16,2,256]{3,2,1,0:T(2,128)S(1)}, f32[3,16,2,256]{3,2,1,0:T(2,128)S(1)}, u32[]{:S(2)}, u32[]{:S(2)}) collective-permute-start(f32[3,16,2,256]{3,2,1,0:T(2,128)S(1)} %get-tuple-element.34), channel_id=1, source_target_pairs={{0,16},{1,2},{2,1},{3,4},{4,3},{5,6},{6,5},{7,8},{8,7},{9,10},{10,... | collective-permute-start | bytes 294920 | tf_op jit(solution)/shard_map/ppermute | solution.py:405
  35.4 4.9 %copy-start.3 = (f32[16,32,256]{2,1,0:T(8,128)S(1)}, f32[16,32,256]{2,1,0:T(8,128)}, u32[]{:S(2)}) copy-start(f32[16,32,256]{2,1,0:T(8,128)} %viscosity_ref.3) | copy-start | bytes 1572868
